TPU v7x, 256 devices: a whole 4x4x8 slice. The times are simulated.
256 devices in a mesh: depth: 4 (over z_hi), gx: 16 (over z_lo, y, core), gy: 4 (over x).
Axes of the slice: x: 4, y: 4, z: 8 (z_hi: 4, z_lo: 2; z = z_hi * 2 + z_lo), core: 2. Of those that a mesh axis runs over, the one named last changes fastest.
Arguments:
- source: float32 [8, 2, 4, 1024, 512], P('depth', None, None, 'gx', 'gy'), may hold values from -6 to 6
- observed: float32 [8, 2, 4, 1024, 512], P('depth', None, None, 'gx', 'gy'), may hold values from -8 to 8
- wavenumber: float32 [8, 1024, 512], P('depth', 'gx', 'gy'), may hold values from 0.5 to 1.5
- damping: float32 [8, 1024, 512], P('depth', 'gx', 'gy'), may hold values from 0.5 to 2
Outputs:
- forward_field: float32 [8, 2, 4, 1024, 512], P('depth', None, None, 'gx', 'gy')
- gradient: float32 [8, 1024, 512], P('depth', 'gx', 'gy')
All inputs are finite; a program needn't handle non-finite values.
Results may differ from a plain program's by a relative error of at most 0.00002.
Values sent between devices are 32-bit elements; how exact they have to be, the bound alone decides.
A program may use at most 64 MiB of HBM per device.

v0:
```python
import jax
import jax.numpy as jnp
from jax import lax
from jax.sharding import PartitionSpec as P


def with_halo(cells, sides, width):
    for axis, dim in sides:
        count = lax.axis_size(axis)
        ends = count - 1
        head = lax.slice_in_dim(cells, 0, width, axis=dim)
        tail = lax.slice_in_dim(cells, cells.shape[dim] - width, cells.shape[dim], axis=dim)
        cells = jnp.concatenate(
            [
                lax.ppermute(tail, axis, [(i, (i + 1) % count) for i in range(ends)]),
                cells,
                lax.ppermute(head, axis, [((i + 1) % count, i) for i in range(ends)]),
            ],
            axis=dim,
        )
    return cells


def shifted(block, axis, distance):
    devices = range(lax.axis_size(axis))
    route = [(i - distance, i) for i in devices if i - distance in devices]
    return lax.ppermute(block, axis, route)


def complex_scale(plane, inverse):
    real_part = inverse[0][None]
    imag_part = inverse[1][None]
    return jnp.stack(
        [plane[0] * real_part - plane[1] * imag_part, plane[0] * imag_part + plane[1] * real_part]
    )


def relax(drive, inverse, edges):
    field = complex_scale(drive, inverse)
    for sweep_step in range(2):
        padded = edges(field)
        beside = (
            padded[:, :, 2:, 1:-1]
            + padded[:, :, :-2, 1:-1]
            + padded[:, :, 1:-1, 2:]
            + padded[:, :, 1:-1, :-2]
        )
        field = complex_scale(drive + beside, inverse)
    return field


def sweep(drive, inverse, incoming, edges, reverse):

    def advance(carry, items):
        plane, inv_plane = items
        result = relax(plane + 2.5 * carry, inv_plane, edges)
        return (result, result)

    final, fields = lax.scan(advance, incoming, (drive, inverse), reverse=reverse)
    return fields


def edges_many(field):
    return with_halo(field, (("gx", 2), ("gy", 3)), 1)


def inverse_pair(wavenumber, damping):
    real_diag = 6.0 - wavenumber
    denom = real_diag * real_diag + damping * damping
    inv_real = real_diag / denom
    inv_imag = damping / denom
    return (jnp.stack([inv_real, -inv_imag], axis=1), jnp.stack([inv_real, inv_imag], axis=1))


def body(source, observed, wavenumber, damping):
    ndepth = lax.axis_size("depth")
    inv_fwd, inv_adj = inverse_pair(wavenumber, damping)
    incoming = jnp.zeros(source.shape[1:], jnp.float32)
    for round_idx in range(ndepth):
        forward_field = sweep(source, inv_fwd, incoming, edges_many, False)
        if round_idx + 1 < ndepth:
            incoming = shifted(forward_field[-1], "depth", 1)
    residual = forward_field - observed
    incoming = jnp.zeros(source.shape[1:], jnp.float32)
    for round_idx in range(ndepth):
        adjoint = sweep(residual, inv_adj, incoming, edges_many, True)
        if round_idx + 1 < ndepth:
            incoming = shifted(adjoint[0], "depth", -1)
    product = forward_field[:, 0] * adjoint[:, 0] + forward_field[:, 1] * adjoint[:, 1]
    gradient = jnp.mean(product, axis=1)
    return (forward_field, gradient)


def solution(mesh):
    return jax.shard_map(
        body,
        mesh=mesh,
        in_specs=(
            P("depth", None, None, "gx", "gy"),
            P("depth", None, None, "gx", "gy"),
            P("depth", "gx", "gy"),
            P("depth", "gx", "gy"),
        ),
        out_specs=(P("depth", None, None, "gx", "gy"), P("depth", "gx", "gy")),
        check_vma=False,
    )
```

profile of v0, /device:TPU:1, one launch (start us, length us, event | category | flops | bytes accessed | tf_op | source)
XLA Modules:
  0.0 723.0 jit_solution(10664219036227395093)
XLA Ops:
  2.6 82.4 %while.112 = (s32[]{:T(128)}, f32[2,4,64,128]{3,2,1,0:T(8,128)S(1)}, f32[2,2,4,64,128]{4,3,2,1,0:T(8,128)S(1)}, f32[2,2,4,64,128]{4,3,2,1,0:T(8,128)S(1)}, f32[2...) while((s32[]{:T(128)}, f32[2,4,64,128]{3,2,1,0:T(8,128)S(1)}, ...), condition=%wide.region_1.2_spmd, body=%wide.region_0.1_spmd.sunk | while | flops 3293187 | bytes 6809785 | solution.py:59
  95.2 82.6 %while.113 = (s32[]{:T(128)}, f32[2,4,64,128]{3,2,1,0:T(8,128)S(1)}, f32[2,2,4,64,128]{4,3,2,1,0:T(8,128)S(1)}, f32[2,2,4,64,128]{4,3,2,1,0:T(8,128)S(1)}, f32[2...) while((s32[]{:T(128)}, f32[2,4,64,128]{3,2,1,0:T(8,128)S(1)}, ...), condition=%wide.region_3.4_spmd, body=%wide.region_2.3_spmd.sunk | while | flops 3293187 | bytes 6809785 | solution.py:59
  97.3 7.8 %collective-permute-start.9 = (f32[2,4,1,128]{3,2,1,0:T(1,128)S(1)}, f32[2,4,1,128]{3,2,1,0:T(1,128)S(1)}, u32[]{:S(2)}, u32[]{:S(2)}) collective-permute-start(f32[2,4,1,128]{3,2,1,0:T(1,128)S(1)} %get-tuple-element.1163), channel_id=1, source_target_pairs={{0,4},{4,8},{8,12},{12,16},{16,20},{20,24},{24,28},{28,32},{32,36}... | collective-permute-start | bytes 12296 | tf_op jit(solution)/shard_map/while/body/eval_jaxpr/ppermute | solution.py:15
  118.0 7.2 collective-permute-start.13
  137.9 8.2 %collective-permute-start.9 = (f32[2,4,1,128]{3,2,1,0:T(1,128)S(1)}, f32[2,4,1,128]{3,2,1,0:T(1,128)S(1)}, u32[]{:S(2)}, u32[]{:S(2)}) collective-permute-start(f32[2,4,1,128]{3,2,1,0:T(1,128)S(1)} %get-tuple-element.1163), channel_id=1, source_target_pairs={{0,4},{4,8},{8,12},{12,16},{16,20},{20,24},{24,28},{28,32},{32,36}... | collective-permute-start | bytes 12296 | tf_op jit(solution)/shard_map/while/body/eval_jaxpr/ppermute | solution.py:15
  158.7 8.5 %collective-permute-start.13 = (f32[2,4,1,128]{3,2,1,0:T(1,128)S(1)}, f32[2,4,1,128]{3,2,1,0:T(1,128)S(1)}, u32[]{:S(2)}, u32[]{:S(2)}) collective-permute-start(f32[2,4,1,128]{3,2,1,0:T(1,128)S(1)} %get-tuple-element.1169), channel_id=1, source_target_pairs={{0,4},{4,8},{8,12},{12,16},{16,20},{20,24},{24,28},{28,32},{32,36}... | collective-permute-start | bytes 12296 | tf_op jit(solution)/shard_map/while/body/eval_jaxpr/ppermute | solution.py:15
  187.4 81.2 %while.114 = (s32[]{:T(128)}, f32[2,4,64,128]{3,2,1,0:T(8,128)S(1)}, f32[2,2,4,64,128]{4,3,2,1,0:T(8,128)S(1)}, f32[2,2,4,64,128]{4,3,2,1,0:T(8,128)S(1)}, f32[2...) while((s32[]{:T(128)}, f32[2,4,64,128]{3,2,1,0:T(8,128)S(1)}, ...), condition=%wide.region_5.6_spmd, body=%wide.region_4.5_spmd.sunk | while | flops 3293187 | bytes 6809785 | solution.py:59
  189.5 8.9 %collective-permute-start.17 = (f32[2,4,1,128]{3,2,1,0:T(1,128)S(1)}, f32[2,4,1,128]{3,2,1,0:T(1,128)S(1)}, u32[]{:S(2)}, u32[]{:S(2)}) collective-permute-start(f32[2,4,1,128]{3,2,1,0:T(1,128)S(1)} %get-tuple-element.1186), channel_id=1, source_target_pairs={{0,4},{4,8},{8,12},{12,16},{16,20},{20,24},{24,28},{28,32},{32,36}... | collective-permute-start | bytes 12296 | tf_op jit(solution)/shard_map/while/body/eval_jaxpr/ppermute | solution.py:15
  230.5 8.0 %collective-permute-start.17 = (f32[2,4,1,128]{3,2,1,0:T(1,128)S(1)}, f32[2,4,1,128]{3,2,1,0:T(1,128)S(1)}, u32[]{:S(2)}, u32[]{:S(2)}) collective-permute-start(f32[2,4,1,128]{3,2,1,0:T(1,128)S(1)} %get-tuple-element.1186), channel_id=1, source_target_pairs={{0,4},{4,8},{8,12},{12,16},{16,20},{20,24},{24,28},{28,32},{32,36}... | collective-permute-start | bytes 12296 | tf_op jit(solution)/shard_map/while/body/eval_jaxpr/ppermute | solution.py:15
  251.1 6.8 collective-permute-start.21
  268.6 7.3 %collective-permute-start.66 = (f32[2,4,64,128]{3,2,1,0:T(8,128)S(1)}, f32[2,4,64,128]{3,2,1,0:T(8,128)S(1)}, u32[]{:S(2)}, u32[]{:S(2)}) collective-permute-start(f32[2,4,64,128]{3,2,1,0:T(8,128)S(1)} %slice_bitcast_fusion.3), channel_id=1, source_target_pairs={{0,64},{64,128},{128,192},{1,65},{65,129},{129,193},{2,66},{66,130... | collective-permute-start | bytes 786440 | tf_op jit(solution)/shard_map/ppermute | solution.py:27
  279.7 77.2 %while.115 = (s32[]{:T(128)}, f32[2,4,64,128]{3,2,1,0:T(8,128)S(1)}, f32[2,2,4,64,128]{4,3,2,1,0:T(8,128)S(1)}, f32[2,2,4,64,128]{4,3,2,1,0:T(8,128)S(1)}, f32[2...) while((s32[]{:T(128)}, f32[2,4,64,128]{3,2,1,0:T(8,128)S(1)}, ...), condition=%wide.region_7.8_spmd, body=%wide.region_6.7_spmd.sunk | while | flops 3293187 | bytes 6809785 | solution.py:59
  281.8 7.5 %collective-permute-start.25 = (f32[2,4,1,128]{3,2,1,0:T(1,128)S(1)}, f32[2,4,1,128]{3,2,1,0:T(1,128)S(1)}, u32[]{:S(2)}, u32[]{:S(2)}) collective-permute-start(f32[2,4,1,128]{3,2,1,0:T(1,128)S(1)} %get-tuple-element.1209), channel_id=1, source_target_pairs={{0,4},{4,8},{8,12},{12,16},{16,20},{20,24},{24,28},{28,32},{32,36}... | collective-permute-start | bytes 12296 | tf_op jit(solution)/shard_map/while/body/eval_jaxpr/ppermute | solution.py:15
  358.3 79.2 %while.116 = (s32[]{:T(128)}, f32[2,4,64,128]{3,2,1,0:T(8,128)S(1)}, f32[2,2,4,64,128]{4,3,2,1,0:T(8,128)S(1)}, f32[2,2,4,64,128]{4,3,2,1,0:T(8,128)S(1)}, f32[2...) while((s32[]{:T(128)}, f32[2,4,64,128]{3,2,1,0:T(8,128)S(1)}, ...), condition=%wide.region_9.10_spmd, body=%wide.region_8.9_spmd.sunk | while | flops 3293188 | bytes 6809789 | solution.py:59
  379.1 7.4 %collective-permute-start.37 = (f32[2,4,1,128]{3,2,1,0:T(1,128)S(1)}, f32[2,4,1,128]{3,2,1,0:T(1,128)S(1)}, u32[]{:S(2)}, u32[]{:S(2)}) collective-permute-start(f32[2,4,1,128]{3,2,1,0:T(1,128)S(1)} %get-tuple-element.1238), channel_id=1, source_target_pairs={{0,4},{4,8},{8,12},{12,16},{16,20},{20,24},{24,28},{28,32},{32,36}... | collective-permute-start | bytes 12296 | tf_op jit(solution)/shard_map/while/body/eval_jaxpr/ppermute | solution.py:15
  399.3 7.4 %collective-permute-start.33 = (f32[2,4,1,128]{3,2,1,0:T(1,128)S(1)}, f32[2,4,1,128]{3,2,1,0:T(1,128)S(1)}, u32[]{:S(2)}, u32[]{:S(2)}) collective-permute-start(f32[2,4,1,128]{3,2,1,0:T(1,128)S(1)} %get-tuple-element.1232), channel_id=1, source_target_pairs={{0,4},{4,8},{8,12},{12,16},{16,20},{20,24},{24,28},{28,32},{32,36}... | collective-permute-start | bytes 12296 | tf_op jit(solution)/shard_map/while/body/eval_jaxpr/ppermute | solution.py:15
  419.3 7.4 %collective-permute-start.37 = (f32[2,4,1,128]{3,2,1,0:T(1,128)S(1)}, f32[2,4,1,128]{3,2,1,0:T(1,128)S(1)}, u32[]{:S(2)}, u32[]{:S(2)}) collective-permute-start(f32[2,4,1,128]{3,2,1,0:T(1,128)S(1)} %get-tuple-element.1238), channel_id=1, source_target_pairs={{0,4},{4,8},{8,12},{12,16},{16,20},{20,24},{24,28},{28,32},{32,36}... | collective-permute-start | bytes 12296 | tf_op jit(solution)/shard_map/while/body/eval_jaxpr/ppermute | solution.py:15
  438.8 11.7 %collective-permute-done.67 = f32[2,4,64,128]{3,2,1,0:T(8,128)S(1)} collective-permute-done((f32[2,4,64,128]{3,2,1,0:T(8,128)S(1)}, f32[2,4,64,128]{3,2,1,0:T(8,128)S(1)}, u32[]{:S(2)}, u32[]{:S(2)}) %collective-permute-start.67) | collective-permute-done | bytes 262176 | tf_op jit(solution)/shard_map/ppermute | solution.py:27
  450.5 77.3 %while.117 = (s32[]{:T(128)}, f32[2,4,64,128]{3,2,1,0:T(8,128)S(1)}, f32[2,2,4,64,128]{4,3,2,1,0:T(8,128)S(1)}, f32[2,2,4,64,128]{4,3,2,1,0:T(8,128)S(1)}, f32[2...) while((s32[]{:T(128)}, f32[2,4,64,128]{3,2,1,0:T(8,128)S(1)}, ...), condition=%wide.region_11.12_spmd, body=%wide.region_10.11_spmd.sunk | while | flops 3293188 | bytes 6809789 | solution.py:59
  452.6 6.5 collective-permute-start.41
  491.0 7.2 collective-permute-start.41
  510.6 6.9 collective-permute-start.45
  529.4 9.6 %collective-permute-done.68 = f32[2,4,64,128]{3,2,1,0:T(8,128)S(1)} collective-permute-done((f32[2,4,64,128]{3,2,1,0:T(8,128)S(1)}, f32[2,4,64,128]{3,2,1,0:T(8,128)S(1)}, u32[]{:S(2)}, u32[]{:S(2)}) %collective-permute-start.68) | collective-permute-done | bytes 262176 | tf_op jit(solution)/shard_map/ppermute | solution.py:27
  539.0 80.1 %while.118 = (s32[]{:T(128)}, f32[2,4,64,128]{3,2,1,0:T(8,128)S(1)}, f32[2,2,4,64,128]{4,3,2,1,0:T(8,128)S(1)}, f32[2,2,4,64,128]{4,3,2,1,0:T(8,128)S(1)}, f32[2...) while((s32[]{:T(128)}, f32[2,4,64,128]{3,2,1,0:T(8,128)S(1)}, ...), condition=%wide.region_13.14_spmd, body=%wide.region_12.13_spmd.sunk | while | flops 3293188 | bytes 6809789 | solution.py:59
  541.0 7.1 collective-permute-start.49
  579.6 9.3 %collective-permute-start.49 = (f32[2,4,1,128]{3,2,1,0:T(1,128)S(1)}, f32[2,4,1,128]{3,2,1,0:T(1,128)S(1)}, u32[]{:S(2)}, u32[]{:S(2)}) collective-permute-start(f32[2,4,1,128]{3,2,1,0:T(1,128)S(1)} %get-tuple-element.1278), channel_id=1, source_target_pairs={{0,4},{4,8},{8,12},{12,16},{16,20},{20,24},{24,28},{28,32},{32,36}... | collective-permute-start | bytes 12296 | tf_op jit(solution)/shard_map/while/body/eval_jaxpr/ppermute | solution.py:15
  601.5 6.9 collective-permute-start.53
  620.4 18.8 %collective-permute-done.69 = f32[2,4,64,128]{3,2,1,0:T(8,128)S(1)} collective-permute-done((f32[2,4,64,128]{3,2,1,0:T(8,128)S(1)}, f32[2,4,64,128]{3,2,1,0:T(8,128)S(1)}, u32[]{:S(2)}, u32[]{:S(2)}) %collective-permute-start.69) | collective-permute-done | bytes 262176 | tf_op jit(solution)/shard_map/ppermute | solution.py:27
  639.2 83.1 %while.119 = (s32[]{:T(128)}, f32[2,4,64,128]{3,2,1,0:T(8,128)S(1)}, f32[2,2,4,64,128]{4,3,2,1,0:T(8,128)S(1)}, f32[2,2,4,64,128]{4,3,2,1,0:T(8,128)S(1)}, f32[2...) while((s32[]{:T(128)}, f32[2,4,64,128]{3,2,1,0:T(8,128)S(1)}, ...), condition=%wide.region_15.16_spmd, body=%wide.region_14.15_spmd.sunk | while | flops 3293188 | bytes 6809789 | solution.py:59
  641.3 9.4 %collective-permute-start.57 = (f32[2,4,1,128]{3,2,1,0:T(1,128)S(1)}, f32[2,4,1,128]{3,2,1,0:T(1,128)S(1)}, u32[]{:S(2)}, u32[]{:S(2)}) collective-permute-start(f32[2,4,1,128]{3,2,1,0:T(1,128)S(1)} %get-tuple-element.1301), channel_id=1, source_target_pairs={{0,4},{4,8},{8,12},{12,16},{16,20},{20,24},{24,28},{28,32},{32,36}... | collective-permute-start | bytes 12296 | tf_op jit(solution)/shard_map/while/body/eval_jaxpr/ppermute | solution.py:15
  664.2 7.3 %collective-permute-start.61 = (f32[2,4,1,128]{3,2,1,0:T(1,128)S(1)}, f32[2,4,1,128]{3,2,1,0:T(1,128)S(1)}, u32[]{:S(2)}, u32[]{:S(2)}) collective-permute-start(f32[2,4,1,128]{3,2,1,0:T(1,128)S(1)} %get-tuple-element.1307), channel_id=1, source_target_pairs={{0,4},{4,8},{8,12},{12,16},{16,20},{20,24},{24,28},{28,32},{32,36}... | collective-permute-start | bytes 12296 | tf_op jit(solution)/shard_map/while/body/eval_jaxpr/ppermute | solution.py:15
  703.2 8.4 %collective-permute-start.61 = (f32[2,4,1,128]{3,2,1,0:T(1,128)S(1)}, f32[2,4,1,128]{3,2,1,0:T(1,128)S(1)}, u32[]{:S(2)}, u32[]{:S(2)}) collective-permute-start(f32[2,4,1,128]{3,2,1,0:T(1,128)S(1)} %get-tuple-element.1307), channel_id=1, source_target_pairs={{0,4},{4,8},{8,12},{12,16},{16,20},{20,24},{24,28},{28,32},{32,36}... | collective-permute-start | bytes 12296 | tf_op jit(solution)/shard_map/while/body/eval_jaxpr/ppermute | solution.py:15
  (495 shorter events, 517.9 us)
Async XLA Ops:
  13.3 10.8 %collective-permute-start.3 = (f32[2,4,66,1]{3,2,1,0:T(8,128)S(1)}, f32[2,4,66,1]{3,2,1,0:T(8,128)S(1)}, u32[]{:S(2)}, u32[]{:S(2)}) collective-permute-start(f32[2,4,66,1]{3,2,1,0:T(8,128)S(1)} %get-tuple-element.1142), channel_id=1, source_target_pairs={{1,0},{2,1},{3,2},{5,4},{6,5},{7,6},{9,8},{10,9},{11,10},{13,12},{... | collective-permute-start | bytes 6344 | tf_op jit(solution)/shard_map/while/body/eval_jaxpr/ppermute | solution.py:17
  30.9 9.7 %collective-permute-start.6 = (f32[2,4,66,1]{3,2,1,0:T(8,128)S(1)}, f32[2,4,66,1]{3,2,1,0:T(8,128)S(1)}, u32[]{:S(2)}, u32[]{:S(2)}) collective-permute-start(f32[2,4,66,1]{3,2,1,0:T(8,128)S(1)} %get-tuple-element.1147), channel_id=1, source_target_pairs={{0,1},{1,2},{2,3},{4,5},{5,6},{6,7},{8,9},{9,10},{10,11},{12,13},{... | collective-permute-start | bytes 6344 | tf_op jit(solution)/shard_map/while/body/eval_jaxpr/ppermute | solution.py:15
  34.1 10.8 %collective-permute-start.7 = (f32[2,4,66,1]{3,2,1,0:T(8,128)S(1)}, f32[2,4,66,1]{3,2,1,0:T(8,128)S(1)}, u32[]{:S(2)}, u32[]{:S(2)}) collective-permute-start(f32[2,4,66,1]{3,2,1,0:T(8,128)S(1)} %get-tuple-element.1148), channel_id=1, source_target_pairs={{1,0},{2,1},{3,2},{5,4},{6,5},{7,6},{9,8},{10,9},{11,10},{13,12},{... | collective-permute-start | bytes 6344 | tf_op jit(solution)/shard_map/while/body/eval_jaxpr/ppermute | solution.py:17
  51.9 9.4 %collective-permute-start.2 = (f32[2,4,66,1]{3,2,1,0:T(8,128)S(1)}, f32[2,4,66,1]{3,2,1,0:T(8,128)S(1)}, u32[]{:S(2)}, u32[]{:S(2)}) collective-permute-start(f32[2,4,66,1]{3,2,1,0:T(8,128)S(1)} %get-tuple-element.1141), channel_id=1, source_target_pairs={{0,1},{1,2},{2,3},{4,5},{5,6},{6,7},{8,9},{9,10},{10,11},{12,13},{... | collective-permute-start | bytes 6344 | tf_op jit(solution)/shard_map/while/body/eval_jaxpr/ppermute | solution.py:15
  54.7 10.9 %collective-permute-start.3 = (f32[2,4,66,1]{3,2,1,0:T(8,128)S(1)}, f32[2,4,66,1]{3,2,1,0:T(8,128)S(1)}, u32[]{:S(2)}, u32[]{:S(2)}) collective-permute-start(f32[2,4,66,1]{3,2,1,0:T(8,128)S(1)} %get-tuple-element.1142), channel_id=1, source_target_pairs={{1,0},{2,1},{3,2},{5,4},{6,5},{7,6},{9,8},{10,9},{11,10},{13,12},{... | collective-permute-start | bytes 6344 | tf_op jit(solution)/shard_map/while/body/eval_jaxpr/ppermute | solution.py:17
  85.0 10.2 %collective-permute-start.64 = (f32[2,4,64,128]{3,2,1,0:T(8,128)S(1)}, f32[2,4,64,128]{3,2,1,0:T(8,128)S(1)}, u32[]{:S(2)}, u32[]{:S(2)}) collective-permute-start(f32[2,4,64,128]{3,2,1,0:T(8,128)S(1)} %slice_bitcast_fusion.5), channel_id=1, source_target_pairs={{0,64},{64,128},{128,192},{1,65},{65,129},{129,193},{2,66},{66,130... | collective-permute-start | bytes 786440 | tf_op jit(solution)/shard_map/ppermute | solution.py:27
  95.4 9.7 %collective-permute-start.8 = (f32[2,4,1,128]{3,2,1,0:T(1,128)S(1)}, f32[2,4,1,128]{3,2,1,0:T(1,128)S(1)}, u32[]{:S(2)}, u32[]{:S(2)}) collective-permute-start(f32[2,4,1,128]{3,2,1,0:T(1,128)S(1)} %get-tuple-element.1162), channel_id=1, source_target_pairs={{4,0},{8,4},{12,8},{16,12},{20,16},{24,20},{28,24},{32,28},{36,32}... | collective-permute-start | bytes 12296 | tf_op jit(solution)/shard_map/while/body/eval_jaxpr/ppermute | solution.py:17
  116.0 9.1 %collective-permute-start.12 = (f32[2,4,1,128]{3,2,1,0:T(1,128)S(1)}, f32[2,4,1,128]{3,2,1,0:T(1,128)S(1)}, u32[]{:S(2)}, u32[]{:S(2)}) collective-permute-start(f32[2,4,1,128]{3,2,1,0:T(1,128)S(1)} %get-tuple-element.1168), channel_id=1, source_target_pairs={{4,0},{8,4},{12,8},{16,12},{20,16},{24,20},{28,24},{32,28},{36,32}... | collective-permute-start | bytes 12296 | tf_op jit(solution)/shard_map/while/body/eval_jaxpr/ppermute | solution.py:17
  136.0 10.1 %collective-permute-start.8 = (f32[2,4,1,128]{3,2,1,0:T(1,128)S(1)}, f32[2,4,1,128]{3,2,1,0:T(1,128)S(1)}, u32[]{:S(2)}, u32[]{:S(2)}) collective-permute-start(f32[2,4,1,128]{3,2,1,0:T(1,128)S(1)} %get-tuple-element.1162), channel_id=1, source_target_pairs={{4,0},{8,4},{12,8},{16,12},{20,16},{24,20},{28,24},{32,28},{36,32}... | collective-permute-start | bytes 12296 | tf_op jit(solution)/shard_map/while/body/eval_jaxpr/ppermute | solution.py:17
  156.8 10.4 %collective-permute-start.12 = (f32[2,4,1,128]{3,2,1,0:T(1,128)S(1)}, f32[2,4,1,128]{3,2,1,0:T(1,128)S(1)}, u32[]{:S(2)}, u32[]{:S(2)}) collective-permute-start(f32[2,4,1,128]{3,2,1,0:T(1,128)S(1)} %get-tuple-element.1168), channel_id=1, source_target_pairs={{4,0},{8,4},{12,8},{16,12},{20,16},{24,20},{28,24},{32,28},{36,32}... | collective-permute-start | bytes 12296 | tf_op jit(solution)/shard_map/while/body/eval_jaxpr/ppermute | solution.py:17
  158.7 9.2 %collective-permute-start.13 = (f32[2,4,1,128]{3,2,1,0:T(1,128)S(1)}, f32[2,4,1,128]{3,2,1,0:T(1,128)S(1)}, u32[]{:S(2)}, u32[]{:S(2)}) collective-permute-start(f32[2,4,1,128]{3,2,1,0:T(1,128)S(1)} %get-tuple-element.1169), channel_id=1, source_target_pairs={{0,4},{4,8},{8,12},{12,16},{16,20},{20,24},{24,28},{28,32},{32,36}... | collective-permute-start | bytes 12296 | tf_op jit(solution)/shard_map/while/body/eval_jaxpr/ppermute | solution.py:15
  177.9 9.4 %collective-permute-start.65 = (f32[2,4,64,128]{3,2,1,0:T(8,128)S(1)}, f32[2,4,64,128]{3,2,1,0:T(8,128)S(1)}, u32[]{:S(2)}, u32[]{:S(2)}) collective-permute-start(f32[2,4,64,128]{3,2,1,0:T(8,128)S(1)} %slice_bitcast_fusion.4), channel_id=1, source_target_pairs={{0,64},{64,128},{128,192},{1,65},{65,129},{129,193},{2,66},{66,130... | collective-permute-start | bytes 786440 | tf_op jit(solution)/shard_map/ppermute | solution.py:27
  187.5 10.8 %collective-permute-start.16 = (f32[2,4,1,128]{3,2,1,0:T(1,128)S(1)}, f32[2,4,1,128]{3,2,1,0:T(1,128)S(1)}, u32[]{:S(2)}, u32[]{:S(2)}) collective-permute-start(f32[2,4,1,128]{3,2,1,0:T(1,128)S(1)} %get-tuple-element.1185), channel_id=1, source_target_pairs={{4,0},{8,4},{12,8},{16,12},{20,16},{24,20},{28,24},{32,28},{36,32}... | collective-permute-start | bytes 12296 | tf_op jit(solution)/shard_map/while/body/eval_jaxpr/ppermute | solution.py:17
  189.5 9.6 %collective-permute-start.17 = (f32[2,4,1,128]{3,2,1,0:T(1,128)S(1)}, f32[2,4,1,128]{3,2,1,0:T(1,128)S(1)}, u32[]{:S(2)}, u32[]{:S(2)}) collective-permute-start(f32[2,4,1,128]{3,2,1,0:T(1,128)S(1)} %get-tuple-element.1186), channel_id=1, source_target_pairs={{0,4},{4,8},{8,12},{12,16},{16,20},{20,24},{24,28},{28,32},{32,36}... | collective-permute-start | bytes 12296 | tf_op jit(solution)/shard_map/while/body/eval_jaxpr/ppermute | solution.py:15
  228.5 9.9 %collective-permute-start.16 = (f32[2,4,1,128]{3,2,1,0:T(1,128)S(1)}, f32[2,4,1,128]{3,2,1,0:T(1,128)S(1)}, u32[]{:S(2)}, u32[]{:S(2)}) collective-permute-start(f32[2,4,1,128]{3,2,1,0:T(1,128)S(1)} %get-tuple-element.1185), channel_id=1, source_target_pairs={{4,0},{8,4},{12,8},{16,12},{20,16},{24,20},{28,24},{32,28},{36,32}... | collective-permute-start | bytes 12296 | tf_op jit(solution)/shard_map/while/body/eval_jaxpr/ppermute | solution.py:17
  268.6 11.0 %collective-permute-start.66 = (f32[2,4,64,128]{3,2,1,0:T(8,128)S(1)}, f32[2,4,64,128]{3,2,1,0:T(8,128)S(1)}, u32[]{:S(2)}, u32[]{:S(2)}) collective-permute-start(f32[2,4,64,128]{3,2,1,0:T(8,128)S(1)} %slice_bitcast_fusion.3), channel_id=1, source_target_pairs={{0,64},{64,128},{128,192},{1,65},{65,129},{129,193},{2,66},{66,130... | collective-permute-start | bytes 786440 | tf_op jit(solution)/shard_map/ppermute | solution.py:27
  279.8 9.4 %collective-permute-start.24 = (f32[2,4,1,128]{3,2,1,0:T(1,128)S(1)}, f32[2,4,1,128]{3,2,1,0:T(1,128)S(1)}, u32[]{:S(2)}, u32[]{:S(2)}) collective-permute-start(f32[2,4,1,128]{3,2,1,0:T(1,128)S(1)} %get-tuple-element.1208), channel_id=1, source_target_pairs={{4,0},{8,4},{12,8},{16,12},{20,16},{24,20},{28,24},{32,28},{36,32}... | collective-permute-start | bytes 12296 | tf_op jit(solution)/shard_map/while/body/eval_jaxpr/ppermute | solution.py:17
  377.2 9.3 %collective-permute-start.36 = (f32[2,4,1,128]{3,2,1,0:T(1,128)S(1)}, f32[2,4,1,128]{3,2,1,0:T(1,128)S(1)}, u32[]{:S(2)}, u32[]{:S(2)}) collective-permute-start(f32[2,4,1,128]{3,2,1,0:T(1,128)S(1)} %get-tuple-element.1237), channel_id=1, source_target_pairs={{4,0},{8,4},{12,8},{16,12},{20,16},{24,20},{28,24},{32,28},{36,32}... | collective-permute-start | bytes 12296 | tf_op jit(solution)/shard_map/while/body/eval_jaxpr/ppermute | solution.py:17
  397.3 9.4 %collective-permute-start.32 = (f32[2,4,1,128]{3,2,1,0:T(1,128)S(1)}, f32[2,4,1,128]{3,2,1,0:T(1,128)S(1)}, u32[]{:S(2)}, u32[]{:S(2)}) collective-permute-start(f32[2,4,1,128]{3,2,1,0:T(1,128)S(1)} %get-tuple-element.1231), channel_id=1, source_target_pairs={{4,0},{8,4},{12,8},{16,12},{20,16},{24,20},{28,24},{32,28},{36,32}... | collective-permute-start | bytes 12296 | tf_op jit(solution)/shard_map/while/body/eval_jaxpr/ppermute | solution.py:17
  417.4 9.4 %collective-permute-start.36 = (f32[2,4,1,128]{3,2,1,0:T(1,128)S(1)}, f32[2,4,1,128]{3,2,1,0:T(1,128)S(1)}, u32[]{:S(2)}, u32[]{:S(2)}) collective-permute-start(f32[2,4,1,128]{3,2,1,0:T(1,128)S(1)} %get-tuple-element.1237), channel_id=1, source_target_pairs={{4,0},{8,4},{12,8},{16,12},{20,16},{24,20},{28,24},{32,28},{36,32}... | collective-permute-start | bytes 12296 | tf_op jit(solution)/shard_map/while/body/eval_jaxpr/ppermute | solution.py:17
  437.5 13.0 %collective-permute-start.67 = (f32[2,4,64,128]{3,2,1,0:T(8,128)S(1)}, f32[2,4,64,128]{3,2,1,0:T(8,128)S(1)}, u32[]{:S(2)}, u32[]{:S(2)}) collective-permute-start(f32[2,4,64,128]{3,2,1,0:T(8,128)S(1)} %slice_bitcast_fusion.2), channel_id=1, source_target_pairs={{64,0},{128,64},{192,128},{65,1},{129,65},{193,129},{66,2},{130,66... | collective-permute-start | bytes 786440 | tf_op jit(solution)/shard_map/ppermute | solution.py:27
  489.1 9.1 %collective-permute-start.40 = (f32[2,4,1,128]{3,2,1,0:T(1,128)S(1)}, f32[2,4,1,128]{3,2,1,0:T(1,128)S(1)}, u32[]{:S(2)}, u32[]{:S(2)}) collective-permute-start(f32[2,4,1,128]{3,2,1,0:T(1,128)S(1)} %get-tuple-element.1254), channel_id=1, source_target_pairs={{4,0},{8,4},{12,8},{16,12},{20,16},{24,20},{28,24},{32,28},{36,32}... | collective-permute-start | bytes 12296 | tf_op jit(solution)/shard_map/while/body/eval_jaxpr/ppermute | solution.py:17
  527.9 11.0 %collective-permute-start.68 = (f32[2,4,64,128]{3,2,1,0:T(8,128)S(1)}, f32[2,4,64,128]{3,2,1,0:T(8,128)S(1)}, u32[]{:S(2)}, u32[]{:S(2)}) collective-permute-start(f32[2,4,64,128]{3,2,1,0:T(8,128)S(1)} %slice_bitcast_fusion.1), channel_id=1, source_target_pairs={{64,0},{128,64},{192,128},{65,1},{129,65},{193,129},{66,2},{130,66... | collective-permute-start | bytes 786440 | tf_op jit(solution)/shard_map/ppermute | solution.py:27
  539.1 9.0 %collective-permute-start.48 = (f32[2,4,1,128]{3,2,1,0:T(1,128)S(1)}, f32[2,4,1,128]{3,2,1,0:T(1,128)S(1)}, u32[]{:S(2)}, u32[]{:S(2)}) collective-permute-start(f32[2,4,1,128]{3,2,1,0:T(1,128)S(1)} %get-tuple-element.1277), channel_id=1, source_target_pairs={{4,0},{8,4},{12,8},{16,12},{20,16},{24,20},{28,24},{32,28},{36,32}... | collective-permute-start | bytes 12296 | tf_op jit(solution)/shard_map/while/body/eval_jaxpr/ppermute | solution.py:17
  577.7 11.2 %collective-permute-start.48 = (f32[2,4,1,128]{3,2,1,0:T(1,128)S(1)}, f32[2,4,1,128]{3,2,1,0:T(1,128)S(1)}, u32[]{:S(2)}, u32[]{:S(2)}) collective-permute-start(f32[2,4,1,128]{3,2,1,0:T(1,128)S(1)} %get-tuple-element.1277), channel_id=1, source_target_pairs={{4,0},{8,4},{12,8},{16,12},{20,16},{24,20},{28,24},{32,28},{36,32}... | collective-permute-start | bytes 12296 | tf_op jit(solution)/shard_map/while/body/eval_jaxpr/ppermute | solution.py:17
  579.6 10.0 %collective-permute-start.49 = (f32[2,4,1,128]{3,2,1,0:T(1,128)S(1)}, f32[2,4,1,128]{3,2,1,0:T(1,128)S(1)}, u32[]{:S(2)}, u32[]{:S(2)}) collective-permute-start(f32[2,4,1,128]{3,2,1,0:T(1,128)S(1)} %get-tuple-element.1278), channel_id=1, source_target_pairs={{0,4},{4,8},{8,12},{12,16},{16,20},{20,24},{24,28},{28,32},{32,36}... | collective-permute-start | bytes 12296 | tf_op jit(solution)/shard_map/while/body/eval_jaxpr/ppermute | solution.py:15
  619.1 20.1 %collective-permute-start.69 = (f32[2,4,64,128]{3,2,1,0:T(8,128)S(1)}, f32[2,4,64,128]{3,2,1,0:T(8,128)S(1)}, u32[]{:S(2)}, u32[]{:S(2)}) collective-permute-start(f32[2,4,64,128]{3,2,1,0:T(8,128)S(1)} %slice_bitcast_fusion), channel_id=1, source_target_pairs={{64,0},{128,64},{192,128},{65,1},{129,65},{193,129},{66,2},{130,66... | collective-permute-start | bytes 786440 | tf_op jit(solution)/shard_map/ppermute | solution.py:27
  639.4 11.3 %collective-permute-start.56 = (f32[2,4,1,128]{3,2,1,0:T(1,128)S(1)}, f32[2,4,1,128]{3,2,1,0:T(1,128)S(1)}, u32[]{:S(2)}, u32[]{:S(2)}) collective-permute-start(f32[2,4,1,128]{3,2,1,0:T(1,128)S(1)} %get-tuple-element.1300), channel_id=1, source_target_pairs={{4,0},{8,4},{12,8},{16,12},{20,16},{24,20},{28,24},{32,28},{36,32}... | collective-permute-start | bytes 12296 | tf_op jit(solution)/shard_map/while/body/eval_jaxpr/ppermute | solution.py:17
  641.3 10.1 %collective-permute-start.57 = (f32[2,4,1,128]{3,2,1,0:T(1,128)S(1)}, f32[2,4,1,128]{3,2,1,0:T(1,128)S(1)}, u32[]{:S(2)}, u32[]{:S(2)}) collective-permute-start(f32[2,4,1,128]{3,2,1,0:T(1,128)S(1)} %get-tuple-element.1301), channel_id=1, source_target_pairs={{0,4},{4,8},{8,12},{12,16},{16,20},{20,24},{24,28},{28,32},{32,36}... | collective-permute-start | bytes 12296 | tf_op jit(solution)/shard_map/while/body/eval_jaxpr/ppermute | solution.py:15
  662.2 9.3 %collective-permute-start.60 = (f32[2,4,1,128]{3,2,1,0:T(1,128)S(1)}, f32[2,4,1,128]{3,2,1,0:T(1,128)S(1)}, u32[]{:S(2)}, u32[]{:S(2)}) collective-permute-start(f32[2,4,1,128]{3,2,1,0:T(1,128)S(1)} %get-tuple-element.1306), channel_id=1, source_target_pairs={{4,0},{8,4},{12,8},{16,12},{20,16},{24,20},{28,24},{32,28},{36,32}... | collective-permute-start | bytes 12296 | tf_op jit(solution)/shard_map/while/body/eval_jaxpr/ppermute | solution.py:17
  701.3 10.3 %collective-permute-start.60 = (f32[2,4,1,128]{3,2,1,0:T(1,128)S(1)}, f32[2,4,1,128]{3,2,1,0:T(1,128)S(1)}, u32[]{:S(2)}, u32[]{:S(2)}) collective-permute-start(f32[2,4,1,128]{3,2,1,0:T(1,128)S(1)} %get-tuple-element.1306), channel_id=1, source_target_pairs={{4,0},{8,4},{12,8},{16,12},{20,16},{24,20},{28,24},{32,28},{36,32}... | collective-permute-start | bytes 12296 | tf_op jit(solution)/shard_map/while/body/eval_jaxpr/ppermute | solution.py:17
  703.2 9.1 %collective-permute-start.61 = (f32[2,4,1,128]{3,2,1,0:T(1,128)S(1)}, f32[2,4,1,128]{3,2,1,0:T(1,128)S(1)}, u32[]{:S(2)}, u32[]{:S(2)}) collective-permute-start(f32[2,4,1,128]{3,2,1,0:T(1,128)S(1)} %get-tuple-element.1307), channel_id=1, source_target_pairs={{0,4},{4,8},{8,12},{12,16},{16,20},{20,24},{24,28},{28,32},{32,36}... | collective-permute-start | bytes 12296 | tf_op jit(solution)/shard_map/while/body/eval_jaxpr/ppermute | solution.py:15
  (104 other events, 1075.0 us)
where the time goes:
time: 737 us; the launch traced here: 723 us
  starting transfers between devices  409 us (55%)
  waiting for transfers between devices  287 us (39%)
  other arithmetic  16.4 us (2%)
    ppermute x64, starting transfers between devices, with_halo(): lax.ppermute(tail, axis, [(i, (i + 1) % count) for i in range(ends)])  279 us
    ppermute x64, waiting for transfers between devices, with_halo(): lax.ppermute(head, axis, [((i + 1) % count, i) for i in range(ends)])  126 us
    ppermute x64, waiting for transfers between devices, with_halo(): lax.ppermute(tail, axis, [(i, (i + 1) % count) for i in range(ends)])  110 us
    ppermute x64, starting transfers between devices, with_halo(): lax.ppermute(head, axis, [((i + 1) % count, i) for i in range(ends)])  107 us
    ppermute x6, waiting for transfers between devices, shifted(): return lax.ppermute(block, axis, route)  52.3 us
    ppermute x6, starting transfers between devices, shifted(): return lax.ppermute(block, axis, route)  22.4 us
  transfers between devices with their start and end apart: 134, of which 102 were waited for; matrix products, arithmetic and copies ran while one was open for 0% of the time, Pallas kernels for 0%

commit v1 on v0

v1 whole, which is shorter than its diff:
```python
import functools

import jax
import jax.numpy as jnp
from jax import lax
from jax.experimental import pallas as pl
from jax.experimental.pallas import tpu as pltpu
from jax.sharding import PartitionSpec as P

MESH = pl.DeviceIdType.MESH
CHUNK = 16
PAD = 8
LANES = 128


def kernel(
    sizes,
    planes,
    halo,
    src,
    obs,
    wavenumber,
    damping,
    fout,
    gout,
    drive,
    cols,
    cols_out,
    observed,
    resid,
    rcols,
    rcols_out,
    field,
    inv_side,
    u0,
    u1,
    u2,
    held,
    prod,
    parts,
    in_send,
    in_recv,
    obs_send,
    obs_recv,
    out_send,
    out_recv,
    grad_send,
    grad_recv,
    row_send,
    row_recv,
    col_send,
    col_recv,
    rrow_send,
    rrow_recv,
    rcol_send,
    rcol_recv,
):
    ndepth, ngx, ngy = sizes
    d = lax.axis_index("depth")
    a = lax.axis_index("gx")
    b = lax.axis_index("gy")
    depth = ndepth * planes
    rows = wavenumber.shape[1]
    ext = rows + 2 * halo
    block = pl.ds(halo, rows)
    mine = pl.ds(planes * d, planes)
    slot = 2 * halo

    up, down = lax.rem(a + ngx - 1, ngx), lax.rem(a + 1, ngx)
    left, right = lax.rem(b + ngy - 1, ngy), lax.rem(b + 1, ngy)
    sideways = [
        {"gx": x, "gy": y}
        for x, y in (
            (up, b),
            (down, b),
            (a, left),
            (a, right),
            (up, left),
            (up, right),
            (down, left),
            (down, right),
        )
    ]
    others = [lax.rem(d + i, ndepth) for i in range(1, ndepth)]
    anyone = {"depth": others[0]}

    def remote(source, target, send, recv, device):
        return pltpu.make_async_remote_copy(
            src_ref=source,
            dst_ref=target,
            send_sem=send,
            recv_sem=recv,
            device_id=device,
            device_id_type=MESH,
        )

    own_source = pltpu.make_async_copy(
        src.at[:, :, d], drive.at[mine, 0:2, block], in_recv.at[d]
    )
    own_source.start()
    pltpu.make_async_copy(obs.at[:, :, d], observed.at[mine], obs_recv.at[d]).start()

    barrier = pltpu.get_barrier_semaphore()
    for device in sideways + [{"depth": e} for e in others]:
        pl.semaphore_signal(barrier, inc=1, device_id=device, device_id_type=MESH)

    for p in range(planes):
        real_diag = 6.0 - wavenumber[p]
        damp = damping[p]
        denom = real_diag * real_diag + damp * damp
        drive[planes * d + p, 2, halo : halo + rows] = real_diag / denom
        drive[planes * d + p, 3, halo : halo + rows] = -damp / denom
    for u in (u0, u1, u2):
        u[...] = jnp.zeros_like(u)

    pl.semaphore_wait(barrier, len(sideways) + len(others))

    for i, e in enumerate(others):
        remote(
            src.at[:, :, e], drive.at[mine, 0:2, block], in_send.at[0, i], in_recv.at[d], {"depth": e}
        ).start()
        remote(
            drive.at[mine, 2:4, block],
            drive.at[mine, 2:4, block],
            in_send.at[1, i],
            in_recv.at[d],
            {"depth": e},
        ).start()

    lane = lax.broadcasted_iota(jnp.int32, (rows, LANES), 1)

    def exchange(z, whole, packed, arrived, rsend, rrecv, csend, crecv):
        top, bottom = pl.ds(halo, halo), pl.ds(rows, halo)
        above, below = pl.ds(0, halo), pl.ds(halo + rows, halo)
        first, last = pl.ds(0, halo), pl.ds(rows - halo, halo)
        for device, source, target in (
            (sideways[0], top, below),
            (sideways[1], bottom, above),
        ):
            remote(
                whole.at[z, :, source], whole.at[z, :, target], rsend.at[z], rrecv.at[z], device
            ).start()
        for device, source, side, target in (
            (sideways[2], pl.ds(0, rows), 1, block),
            (sideways[3], pl.ds(0, rows), 0, block),
            (sideways[4], first, 1, below),
            (sideways[5], first, 0, below),
            (sideways[6], last, 1, above),
            (sideways[7], last, 0, above),
        ):
            remote(
                packed.at[z, source],
                arrived.at[z, side, target],
                csend.at[z],
                crecv.at[z],
                device,
            ).start()

    def pack(pieces):
        out = pieces[0]
        for k in range(1, len(pieces)):
            here = (lane >= slot * k - halo) & (lane < slot * k + halo)
            out = jnp.where(here, pltpu.roll(pieces[k], slot * k, axis=1), out)
        return out

    def spread(e, carry):
        for p in range(planes):
            z = planes * e + p
            cols_out[z] = pack([drive[z, k, halo : halo + rows] for k in range(4)])
            exchange(z, drive, cols_out, cols, row_send, row_recv, col_send, col_recv)
        return carry

    own_source.wait()
    spread(d, 0)

    def gather(i, carry):
        e = lax.rem(d + i, ndepth)
        whole = drive.at[pl.ds(planes * e, planes), :, block]
        remote(whole, whole, in_send.at[0, 0], in_recv.at[e], anyone).wait_recv()
        return spread(e, carry)

    lax.fori_loop(1, ndepth, gather, 0)

    for i, e in enumerate(others):
        remote(
            obs.at[:, :, e], observed.at[mine], obs_send.at[i], obs_recv.at[d], {"depth": e}
        ).start()

    not_top = (a > 0).astype(jnp.float32)
    not_bottom = (a < ngx - 1).astype(jnp.float32)
    not_left = (b > 0).astype(jnp.float32)
    not_right = (b < ngy - 1).astype(jnp.float32)
    clane = lax.broadcasted_iota(jnp.int32, (CHUNK, LANES), 1)
    inside = jnp.where(
        clane < halo, not_right, jnp.where(clane >= LANES - halo, not_left, 0.0)
    )
    from_right = lax.rem(clane, slot) < halo
    at_first = clane == 0
    at_last = clane == LANES - 1
    chunks = range(0, ext, CHUNK)

    def at(r):
        return slice(PAD + r, PAD + r + CHUNK)

    def unpack(arrived, z, r, count):
        both = jnp.where(
            from_right, arrived[z, 1, r : r + CHUNK], arrived[z, 0, r : r + CHUNK]
        )
        return [both] + [
            pltpu.roll(both, LANES - slot * k, axis=1) for k in range(1, count)
        ]

    def scale(vr, vi, qr, qi, sign):
        if sign > 0:
            return vr * qr - vi * qi, vr * qi + vi * qr
        return vr * qr + vi * qi, vi * qr - vr * qi

    def stencil(u, r):
        sums = []
        for c in range(2):
            vert = [u[c + k, PAD + r - 1 : PAD + r - 1 + CHUNK] + u[c + k, PAD + r + 1 : PAD + r + 1 + CHUNK] for k in (0, 2)]
            mid, side = u[c, at(r)], u[c + 2, at(r)]
            mid_l, mid_r = pltpu.roll(mid, 1, axis=1), pltpu.roll(mid, LANES - 1, axis=1)
            side_l, side_r = pltpu.roll(side, 1, axis=1), pltpu.roll(side, LANES - 1, axis=1)
            in_mid = vert[0] + jnp.where(at_first, side_l, mid_l) + jnp.where(at_last, side_r, mid_r)
            in_side = vert[1] + jnp.where(at_first, mid_l, side_l) + jnp.where(at_last, mid_r, side_r)
            sums.append((in_mid, in_side))
        return [sums[0][0], sums[1][0], sums[0][1], sums[1][1]]

    def inverse_at(z, r):
        span = slice(r, r + CHUNK)
        return drive[z, 2, span], drive[z, 3, span], inv_side[z, 0, span], inv_side[z, 1, span]

    def write(u, r, g, inv, sign):
        mr, mi = scale(g[0], g[1], inv[0], inv[1], sign)
        sr, si = scale(g[2], g[3], inv[2], inv[3], sign)
        for k, v in enumerate((mr, mi, sr, si)):
            u[k, at(r)] = v
        return mr, mi

    def relax(z, sign, finish):
        for source, target in ((u0, u1), (u1, u2)):
            for r in chunks:
                sums = stencil(source, r)
                g = [held[k, r : r + CHUNK] + sums[k] for k in range(4)]
                mr, mi = write(target, r, g, inverse_at(z, r), sign)
                if target is u2 and halo <= r < halo + rows:
                    finish(slice(r - halo, r - halo + CHUNK), mr, mi)

    def forward(z, carry):
        edge = drive.at[z, :, pl.ds(0, 2 * halo)]
        remote(edge, edge, row_send.at[z], row_recv.at[z], anyone).wait_recv()
        remote(cols.at[z], cols.at[z], col_send.at[z], col_recv.at[z], anyone).wait_recv()
        for r in chunks:
            span = slice(r, r + CHUNK)
            piece = unpack(cols, z, r, 4)
            inv = [drive[z, 2, span], drive[z, 3, span], piece[2] * inside, piece[3] * inside]
            if r < halo:
                inv = [q * not_top for q in inv]
            if r >= halo + rows:
                inv = [q * not_bottom for q in inv]
            if r < halo or r >= halo + rows:
                drive[z, 2, span] = inv[0]
                drive[z, 3, span] = inv[1]
            inv_side[z, 0, span] = inv[2]
            inv_side[z, 1, span] = inv[3]
            base = [drive[z, 0, span], drive[z, 1, span], piece[0], piece[1]]
            g = [base[k] + 2.5 * u2[k, at(r)] for k in range(4)]
            for k in range(4):
                held[k, span] = g[k]
            write(u0, r, g, inv, 1)

        def finish(span, mr, mi):
            field[z, 0, span] = mr
            field[z, 1, span] = mi

        relax(z, 1, finish)
        return carry

    lax.fori_loop(0, depth, forward, 0)
    u2[...] = jnp.zeros_like(u2)

    def remain(i, carry):
        e = ndepth - 1 - i
        pair = observed.at[pl.ds(planes * e, planes)]
        remote(pair, pair, obs_send.at[0], obs_recv.at[e], anyone).wait_recv()
        for p in reversed(range(planes)):
            z = planes * e + p
            piece = []
            for c in range(2):
                value = field[z, c] - observed[z, c]
                resid[z, c, halo : halo + rows] = value
                piece.append(value)
            rcols_out[z] = pack(piece)
            exchange(z, resid, rcols_out, rcols, rrow_send, rrow_recv, rcol_send, rcol_recv)
        return carry

    lax.fori_loop(0, ndepth, remain, 0)

    for i, e in enumerate(others):
        theirs = pl.ds(planes * e, planes)
        remote(
            field.at[theirs], fout.at[:, :, d], out_send.at[i], out_recv.at[d], {"depth": e}
        ).start()
    pltpu.make_async_copy(field.at[mine], fout.at[:, :, d], out_recv.at[d]).start()

    def adjoint(i, carry):
        z = depth - 1 - i
        edge = resid.at[z, :, pl.ds(0, 2 * halo)]
        remote(edge, edge, rrow_send.at[z], rrow_recv.at[z], anyone).wait_recv()
        remote(rcols.at[z], rcols.at[z], rcol_send.at[z], rcol_recv.at[z], anyone).wait_recv()
        for r in chunks:
            span = slice(r, r + CHUNK)
            piece = unpack(rcols, z, r, 2)
            base = [resid[z, 0, span], resid[z, 1, span], piece[0], piece[1]]
            g = [base[k] + 2.5 * u2[k, at(r)] for k in range(4)]
            for k in range(4):
                held[k, span] = g[k]
            write(u0, r, g, inverse_at(z, r), -1)

        def finish(span, mr, mi):
            prod[z, span] = field[z, 0, span] * mr + field[z, 1, span] * mi

        relax(z, -1, finish)
        e = z // planes

        @pl.when((z == planes * e) & (e != d))
        def _():
            remote(
                prod.at[pl.ds(z, planes)], parts.at[d], grad_send.at[e], grad_recv.at[d], {"depth": e}
            ).start()

        return carry

    lax.fori_loop(0, depth, adjoint, 0)

    total = prod[mine]
    for e in others:
        remote(parts.at[e], parts.at[e], grad_send.at[e], grad_recv.at[e], anyone).wait_recv()
        total = total + parts[e]
    gout[...] = total * (1.0 / ndepth)

    for i, e in enumerate(others):
        taken = fout.at[:, :, e]
        remote(taken, taken, out_send.at[0], out_recv.at[e], anyone).wait_recv()
    taken = fout.at[:, :, d]
    pltpu.make_async_copy(field.at[mine], taken, out_recv.at[d]).wait()
    for i, e in enumerate(others):
        remote(parts.at[e], parts.at[e], grad_send.at[e], grad_recv.at[e], anyone).wait_send()
        pair = observed.at[mine]
        remote(pair, pair, obs_send.at[i], obs_recv.at[e], anyone).wait_send()
        remote(pair, pair, out_send.at[i], out_recv.at[e], anyone).wait_send()
        for k in range(2):
            remote(pair, pair, in_send.at[k, i], in_recv.at[e], anyone).wait_send()

    def finish_sends(z, carry):
        edge = drive.at[z, :, pl.ds(0, 2 * halo)]
        remote(edge, edge, row_send.at[z], row_recv.at[z], anyone).wait_send()
        remote(cols.at[z], cols.at[z], col_send.at[z], col_recv.at[z], anyone).wait_send()
        edge = resid.at[z, :, pl.ds(0, 2 * halo)]
        remote(edge, edge, rrow_send.at[z], rrow_recv.at[z], anyone).wait_send()
        remote(rcols.at[z], rcols.at[z], rcol_send.at[z], rcol_recv.at[z], anyone).wait_send()
        return carry

    lax.fori_loop(0, depth, finish_sends, 0)


def body(sizes, source, observed, wavenumber, damping):
    planes, comps, shots, rows, lanes = source.shape
    ndepth = sizes[0]
    depth = ndepth * planes
    halo = 2 * depth
    ext = rows + 2 * halo
    assert comps == 2 and shots == ndepth and lanes == LANES and 8 * halo == LANES
    vmem = lambda *shape: pltpu.VMEM(shape, jnp.float32)
    dma = lambda *shape: pltpu.SemaphoreType.DMA(shape)
    anywhere = pl.BlockSpec(memory_space=pl.ANY)
    local = pl.BlockSpec(memory_space=pltpu.VMEM)
    return pl.pallas_call(
        functools.partial(kernel, sizes, planes, halo),
        name="sweeps",
        out_shape=(
            jax.ShapeDtypeStruct(source.shape, jnp.float32),
            jax.ShapeDtypeStruct(wavenumber.shape, jnp.float32),
        ),
        in_specs=[anywhere, anywhere, local, local],
        out_specs=(anywhere, local),
        scratch_shapes=[
            vmem(depth, 4, ext, lanes),
            vmem(depth, 2, ext, lanes),
            vmem(depth, rows, lanes),
            vmem(depth, 2, rows, lanes),
            vmem(depth, 2, ext, lanes),
            vmem(depth, 2, ext, lanes),
            vmem(depth, rows, lanes),
            vmem(depth, 2, rows, lanes),
            vmem(depth, 2, ext, lanes),
            vmem(4, ext + 2 * PAD, lanes),
            vmem(4, ext + 2 * PAD, lanes),
            vmem(4, ext + 2 * PAD, lanes),
            vmem(4, ext, lanes),
            vmem(depth, rows, lanes),
            vmem(ndepth, planes, rows, lanes),
            dma(2, ndepth),
            dma(ndepth),
            dma(ndepth),
            dma(ndepth),
            dma(ndepth),
            dma(ndepth),
            dma(ndepth),
            dma(ndepth),
            dma(depth),
            dma(depth),
            dma(depth),
            dma(depth),
            dma(depth),
            dma(depth),
            dma(depth),
            dma(depth),
        ],
        compiler_params=pltpu.CompilerParams(
            collective_id=0, has_side_effects=True, vmem_limit_bytes=32 << 20
        ),
    )(source, observed, wavenumber, damping)


def solution(mesh):
    sizes = tuple(mesh.shape[axis] for axis in ("depth", "gx", "gy"))
    return jax.shard_map(
        functools.partial(body, sizes),
        mesh=mesh,
        in_specs=(
            P("depth", None, None, "gx", "gy"),
            P("depth", None, None, "gx", "gy"),
            P("depth", "gx", "gy"),
            P("depth", "gx", "gy"),
        ),
        out_specs=(P("depth", None, None, "gx", "gy"), P("depth", "gx", "gy")),
        check_vma=False,
    )
```

time: 737 us -> 81.6 us (0.11); the launches traced: 723 us -> 81.4 us
  starting transfers between devices: 409 us -> 0 us
  waiting for transfers between devices: 287 us -> 0 us
  Pallas kernels: 0 us -> 75.5 us
  other arithmetic: 16.4 us -> 0 us
    ppermute x134 -> x0, starting transfers between devices: 409 us -> none  [the longest x64 279 us: with_halo(): lax.ppermute(tail, axis, [(i, (i + 1) % count) for i in range(ends)])]
    ppermute x134 -> x0, waiting for transfers between devices: 287 us -> none  [the longest x64 126 us: with_halo(): lax.ppermute(head, axis, [((i + 1) % count, i) for i in range(ends)])]
    pallas_call x0 -> x1, Pallas kernels: none -> 75.5 us  [body(): pl.pallas_call(functools.partial(kernel, sizes, planes, halo), name='swee...]
    add x48 -> x0, other arithmetic: 9.86 us -> none  [the longest x32 9.26 us: relax(): field = complex_scale(drive + beside, inverse)]
  transfers between devices with their start and end apart: 134 -> 0, of which waited for: 102 -> 0; matrix products, arithmetic and copies ran while one was open for 0% -> 0% of each run, Pallas kernels for 0% -> 0%
where the time goes in v1:
time: 81.6 us; the launch traced here: 81.4 us
  Pallas kernels  75.5 us (93%)
  local copies, waits for them, and re-layouts  5.18 us (6%)
    pallas_call x1, Pallas kernels, body(): pl.pallas_call(functools.partial(kernel, sizes, planes, halo), name='swee...  75.5 us
    unnamed x10, local copies, waits for them, and re-layouts  5.18 us

profile of v1, /device:TPU:1, one launch (start us, length us, event | category | flops | bytes accessed | tf_op | source)
XLA Modules:
  0.0 81.4 jit_solution(9844102724415344249)
XLA Ops:
  0.6 0.0 copy-start
  0.6 1.0 %copy-done = f32[2,2,4,64,128]{4,3,2,1,0:T(8,128)S(1)} copy-done((f32[2,2,4,64,128]{4,3,2,1,0:T(8,128)S(1)}, f32[2,2,4,64,128]{4,3,2,1,0:T(8,128)}, u32[]{:S(2)}) %copy-start) | copy-done | bytes 524312
  1.7 0.0 copy-start.1
  1.7 1.0 %copy-done.1 = f32[2,2,4,64,128]{4,3,2,1,0:T(8,128)S(1)} copy-done((f32[2,2,4,64,128]{4,3,2,1,0:T(8,128)S(1)}, f32[2,2,4,64,128]{4,3,2,1,0:T(8,128)}, u32[]{:S(2)}) %copy-start.1) | copy-done | bytes 524312
  2.7 0.0 copy-start.2
  2.7 0.8 %copy-done.2 = f32[2,64,128]{2,1,0:T(8,128)S(1)} copy-done((f32[2,64,128]{2,1,0:T(8,128)S(1)}, f32[2,64,128]{2,1,0:T(8,128)}, u32[]{:S(2)}) %copy-start.2) | copy-done | bytes 65560
  3.6 0.0 copy-start.3
  3.6 0.8 %copy-done.3 = f32[2,64,128]{2,1,0:T(8,128)S(1)} copy-done((f32[2,64,128]{2,1,0:T(8,128)S(1)}, f32[2,64,128]{2,1,0:T(8,128)}, u32[]{:S(2)}) %copy-start.3) | copy-done | bytes 65560
  4.4 75.5 %sweeps.1 = (f32[2,2,4,64,128]{4,3,2,1,0:T(8,128)S(1)}, f32[2,64,128]{2,1,0:T(8,128)S(1)}) custom-call(f32[2,2,4,64,128]{4,3,2,1,0:T(8,128)S(1)} %copy-done, f32[2,2,4,64,128]{4,3,2,1,0:T(8,128)S(1)} %copy-done.1, f32[2,64,128]{2,1,0:T(8,128)S(1)} %copy-done.2, f32[2,64,128]{2,1,0:T(8,128)S(1)} %copy-done.3), custom_call_target="tpu_custom_call" | custom-call | tf_op jit(solution)/shard_map/sweeps/pallas_call | solution.py:379
  79.9 0.8 copy.8
  80.7 0.6 copy.9
Async XLA Ops:
  0.6 1.0 %copy-start = (f32[2,2,4,64,128]{4,3,2,1,0:T(8,128)S(1)}, f32[2,2,4,64,128]{4,3,2,1,0:T(8,128)}, u32[]{:S(2)}) copy-start(f32[2,2,4,64,128]{4,3,2,1,0:T(8,128)} %src.1) | copy-start | bytes 1572868
  1.7 1.0 %copy-start.1 = (f32[2,2,4,64,128]{4,3,2,1,0:T(8,128)S(1)}, f32[2,2,4,64,128]{4,3,2,1,0:T(8,128)}, u32[]{:S(2)}) copy-start(f32[2,2,4,64,128]{4,3,2,1,0:T(8,128)} %obs.1) | copy-start | bytes 1572868
  2.7 0.8 %copy-start.2 = (f32[2,64,128]{2,1,0:T(8,128)S(1)}, f32[2,64,128]{2,1,0:T(8,128)}, u32[]{:S(2)}) copy-start(f32[2,64,128]{2,1,0:T(8,128)} %wavenumber.1) | copy-start | bytes 196612
  3.6 0.8 %copy-start.3 = (f32[2,64,128]{2,1,0:T(8,128)S(1)}, f32[2,64,128]{2,1,0:T(8,128)}, u32[]{:S(2)}) copy-start(f32[2,64,128]{2,1,0:T(8,128)} %damping.1) | copy-start | bytes 196612

commit v2 on v0

v2 whole, which is shorter than its diff:
```python
import functools

import jax
import jax.numpy as jnp
from jax import lax
from jax.experimental import pallas as pl
from jax.experimental.pallas import tpu as pltpu
from jax.sharding import PartitionSpec as P

MESH = pl.DeviceIdType.MESH
CHUNK = 16
PAD = 8
LANES = 128
TILE = 8


def kernel(
    sizes,
    halo,
    edge,
    src,
    obs,
    wavenumber,
    damping,
    fout,
    gout,
    data,
    sides,
    folded,
    observed,
    weight,
    carry,
    carry_side,
    leave,
    leave_side,
    result,
    u0,
    u1,
    u2,
    held,
    total,
    other,
    load,
    row_send,
    row_recv,
    side_send,
    side_recv,
    carry_send,
    carry_recv,
    cside_send,
    cside_recv,
    in_send,
    in_recv,
    obs_send,
    obs_recv,
    out_send,
    out_recv,
    grad_send,
    grad_recv,
):
    ndepth, ngx, ngy = sizes
    d = lax.axis_index("depth")
    a = lax.axis_index("gx")
    b = lax.axis_index("gy")
    planes, _, shots, rows, _ = src.shape
    ext = rows + 2 * halo
    block = pl.ds(halo, rows)
    half = lax.rem(d, 2)
    lower = d // 2
    mine = 2 * lax.rem(d + lower, 2)
    theirs = 2 - mine

    def source_group(s, h):
        return 2 * s + h

    def residual_group(s, h):
        return 4 + 2 * s + h

    def inverse_group(h):
        return 8 + h

    up, down = lax.rem(a + ngx - 1, ngx), lax.rem(a + 1, ngx)
    left, right = lax.rem(b + ngy - 1, ngy), lax.rem(b + 1, ngy)
    beside = [
        {"gx": x, "gy": y}
        for x, y in (
            (up, b),
            (down, b),
            (a, left),
            (a, right),
            (up, left),
            (up, right),
            (down, left),
            (down, right),
        )
    ]
    partner = {"depth": d + 1 - 2 * half}
    through = [{"depth": ndepth - 1 - d, "gy": y} for y in (b, left, right)]
    anyone = beside[0]

    def remote(source, target, send, recv, device):
        return pltpu.make_async_remote_copy(
            src_ref=source,
            dst_ref=target,
            send_sem=send,
            recv_sem=recv,
            device_id=device,
            device_id_type=MESH,
        )

    inverse_loads = [
        pltpu.make_async_copy(wavenumber, held.at[0:planes, 0:rows], load.at[0]),
        pltpu.make_async_copy(damping, held.at[planes : 2 * planes, 0:rows], load.at[1]),
    ]
    source_loads, observed_loads = [], []
    for s in range(2):
        for p in range(planes):
            k = 2 + 4 * s + 2 * p
            pair = pl.ds(2 * p, 2)
            source_loads.append(
                pltpu.make_async_copy(
                    src.at[p, :, mine + s], data.at[source_group(s, half), pair, block], load.at[k]
                )
            )
            observed_loads.append(
                pltpu.make_async_copy(
                    obs.at[p, :, mine + s], observed.at[s, half, pair], load.at[k + 1]
                )
            )
    for copy in inverse_loads + source_loads + observed_loads:
        copy.start()

    carry[...] = jnp.zeros_like(carry)
    carry_side[...] = jnp.zeros_like(carry_side)

    barrier = pltpu.get_barrier_semaphore()
    partners = beside + [partner] + through
    for device in partners:
        pl.semaphore_signal(barrier, inc=1, device_id=device, device_id_type=MESH)

    for copy in inverse_loads:
        copy.wait()
    for p in range(planes):
        real_diag = 6.0 - held[p, 0:rows]
        damp = held[planes + p, 0:rows]
        denom = real_diag * real_diag + damp * damp
        data[inverse_group(half), 2 * p, halo : halo + rows] = real_diag / denom
        data[inverse_group(half), 2 * p + 1, halo : halo + rows] = -damp / denom

    pl.semaphore_wait(barrier, len(partners))

    own_inverse = data.at[inverse_group(half), :, block]
    remote(own_inverse, own_inverse, in_send.at[0], in_recv.at[0], partner).start()
    for s in range(2):
        for p in range(planes):
            remote(
                src.at[p, :, theirs + s],
                data.at[source_group(s, half), pl.ds(2 * p, 2), block],
                in_send.at[1 + s],
                in_recv.at[1 + s],
                partner,
            ).start()

    for u in (u0, u1):
        u[...] = jnp.zeros_like(u)
    for k in range(4):
        u2[k, 0:PAD] = jnp.zeros_like(u2[k, 0:PAD])
        u2[k, PAD + ext : 2 * PAD + ext] = jnp.zeros_like(u2[k, 0:PAD])
    total[...] = jnp.zeros_like(total)

    lane = lax.broadcasted_iota(jnp.int32, (TILE, LANES), 1)
    lane_group = lane // edge
    groups = LANES // edge

    def fold(read, count, tiles):
        for_left = for_right = None
        for k in range(tiles):
            for j in range(count):
                at = k * count + j
                moved = pltpu.roll(read(j, k), (edge * (at + 1)) % LANES, axis=1)
                if for_left is None:
                    for_left = for_right = moved
                else:
                    for_left = jnp.where(lane_group == (at + 1) % groups, moved, for_left)
                    for_right = jnp.where(lane_group == at, moved, for_right)
        return for_left, for_right

    def unfold(from_left, from_right, at):
        shift = (LANES - edge * (at + 1)) % LANES
        return jnp.where(
            lane < LANES // 2,
            pltpu.roll(from_right, shift, axis=1),
            pltpu.roll(from_left, shift, axis=1),
        )

    def exchange(g):
        for device, source, target in (
            (beside[0], pl.ds(halo, halo), pl.ds(halo + rows, halo)),
            (beside[1], pl.ds(rows, halo), pl.ds(0, halo)),
        ):
            remote(
                data.at[g, :, source], data.at[g, :, target], row_send.at[g], row_recv.at[g], device
            ).start()
        for p in range(planes):
            for_left, for_right = fold(
                lambda c, k: data[g, 2 * p + c, halo + TILE * k : halo + TILE * k + TILE], 2, rows // TILE
            )
            folded[g, 0, p] = for_left
            folded[g, 1, p] = for_right
        for device, source, side, piece in (
            (beside[2], 0, 1, 1),
            (beside[3], 1, 0, 1),
            (beside[4], 0, 1, 2),
            (beside[5], 1, 0, 2),
            (beside[6], 0, 1, 0),
            (beside[7], 1, 0, 0),
        ):
            remote(
                folded.at[g, source], sides.at[g, side, piece], side_send.at[g], side_recv.at[g], device
            ).start()

    def edges(g):
        return data.at[g, :, pl.ds(0, 2 * halo)]

    def arrive(g):
        remote(edges(g), edges(g), row_send.at[g], row_recv.at[g], anyone).wait_recv()
        remote(sides.at[g], sides.at[g], side_send.at[g], side_recv.at[g], anyone).wait_recv()

    def side_of(g, p, c, t):
        spare = halo // TILE
        inner = rows // TILE
        if t < spare:
            piece, k = 0, t + inner - spare
        elif t < spare + inner:
            piece, k = 1, t - spare
        else:
            piece, k = 2, t - spare - inner
        return unfold(sides[g, 0, piece, p], sides[g, 1, piece, p], 2 * k + c)

    exchange(inverse_group(half))
    for copy in source_loads:
        copy.wait()

    def landed(k, g):
        whole = data.at[g, :, block]
        remote(whole, whole, in_send.at[k], in_recv.at[k], anyone).wait_recv()
        exchange(g)

    def spread(i, c):
        @pl.when(i < 2)
        def _():
            exchange(source_group(i, half))

        @pl.when(i >= 2)
        def _():
            landed(i - 2, jnp.where(i == 2, inverse_group(1 - half), source_group(i - 3, 1 - half)))

        return c

    lax.fori_loop(0, 5, spread, 0)
    for s in range(2):
        for p in range(planes):
            remote(
                obs.at[p, :, theirs + s],
                observed.at[s, half, pl.ds(2 * p, 2)],
                obs_send.at[s],
                obs_recv.at[s],
                partner,
            ).start()

    not_top = (a > 0).astype(jnp.float32)
    not_bottom = (a < ngx - 1).astype(jnp.float32)
    not_left = (b > 0).astype(jnp.float32)
    not_right = (b < ngy - 1).astype(jnp.float32)
    inside = jnp.where(lane < edge, not_right, jnp.where(lane >= LANES - edge, not_left, 0.0))

    def weigh(h, carried):
        g = inverse_group(h)
        arrive(g)
        for p in range(planes):
            z = planes * h + p
            for t in range(ext // TILE):
                span = slice(TILE * t, TILE * t + TILE)
                for c in range(2):
                    mid = data[g, 2 * p + c, span]
                    side = side_of(g, p, c, t) * inside
                    if TILE * t < halo:
                        mid, side = mid * not_top, side * not_top
                    if TILE * t >= halo + rows:
                        mid, side = mid * not_bottom, side * not_bottom
                    weight[0, z, c, span] = mid
                    weight[0, z, 2 + c, span] = side
                    weight[1, z, c, span] = -mid if c else mid
                    weight[1, z, 2 + c, span] = -side if c else side
        return carried

    lax.fori_loop(0, 2, weigh, 0)
    for copy in observed_loads:
        copy.wait()

    clane = lax.broadcasted_iota(jnp.int32, (CHUNK, LANES), 1)
    at_first = clane == 0
    at_last = clane == LANES - 1
    chunks = range(0, ext, CHUNK)

    def at(r):
        return slice(PAD + r, PAD + r + CHUNK)

    def stencil(u, r):
        sums = []
        higher, lower_rows = slice(PAD + r - 1, PAD + r - 1 + CHUNK), slice(PAD + r + 1, PAD + r + 1 + CHUNK)
        for c in range(2):
            mid, side = u[c, at(r)], u[c + 2, at(r)]
            mid_l, mid_r = pltpu.roll(mid, 1, axis=1), pltpu.roll(mid, LANES - 1, axis=1)
            side_l, side_r = pltpu.roll(side, 1, axis=1), pltpu.roll(side, LANES - 1, axis=1)
            in_mid = jnp.where(at_first, side_l, mid_l) + jnp.where(at_last, side_r, mid_r)
            in_side = jnp.where(at_first, mid_l, side_l) + jnp.where(at_last, mid_r, side_r)
            sums.append(
                (
                    in_mid + (u[c, higher] + u[c, lower_rows]),
                    in_side + (u[c + 2, higher] + u[c + 2, lower_rows]),
                )
            )
        return [sums[0][0], sums[1][0], sums[0][1], sums[1][1]]

    def scaled(g, kind, z, r):
        q = [weight[kind, z, k, r : r + CHUNK] for k in range(4)]
        out = []
        for k in (0, 2):
            out.append(g[k] * q[k] - g[k + 1] * q[k + 1])
            out.append(g[k] * q[k + 1] + g[k + 1] * q[k])
        return out

    def relax(kind, s, z):
        for r in chunks:
            v = scaled([held[k, r : r + CHUNK] for k in range(4)], kind, z, r)
            for k in range(4):
                u0[k, at(r)] = v[k]
        for source, target in ((u0, u1), (u1, u2)):
            for r in chunks:
                sums = stencil(source, r)
                v = scaled([held[k, r : r + CHUNK] + sums[k] for k in range(4)], kind, z, r)
                for k in range(4):
                    target[k, at(r)] = v[k]
                if target is u2 and halo <= r < halo + rows:
                    result[kind, s, z, 0, r - halo : r - halo + CHUNK] = v[0]
                    result[kind, s, z, 1, r - halo : r - halo + CHUNK] = v[1]

    most = pl.ds(TILE, ext - 2 * TILE)

    def wait_carry(kind, s):
        @pl.when(kind != lower)
        def _():
            ref = carry_side.at[kind, s]
            remote(ref, ref, cside_send.at[kind, s], cside_recv.at[kind, s], anyone).wait_recv()
            ref = carry.at[kind, s, :, most]
            remote(ref, ref, carry_send.at[kind, s], carry_recv.at[kind, s], anyone).wait_recv()

    def hand_on(kind, s):
        for c in range(2):
            for t in range(ext // TILE):
                leave[kind, s, c, TILE * t : TILE * t + TILE] = u2[c, PAD + TILE * t : PAD + TILE * t + TILE]
            for_left, for_right = fold(
                lambda j, k: u2[c, PAD + TILE * k : PAD + TILE * k + TILE], 1, ext // TILE
            )
            leave_side[kind, s, 0, c] = for_left
            leave_side[kind, s, 1, c] = for_right

        @pl.when(kind == lower)
        def _():
            for source, device in ((0, through[1]), (1, through[2])):
                remote(
                    leave_side.at[kind, s, source],
                    carry_side.at[kind, s, 1 - source],
                    cside_send.at[kind, s],
                    cside_recv.at[kind, s],
                    device,
                ).start()
            remote(
                leave.at[kind, s, :, most],
                carry.at[kind, s, :, most],
                carry_send.at[kind, s],
                carry_recv.at[kind, s],
                through[0],
            ).start()

    def field_out(s, send):
        mine_now = result.at[0, s, pl.ds(planes * (1 - half), planes)]
        return remote(mine_now, fout.at[:, :, mine + s], out_send.at[s], out_recv.at[s], partner)

    def step(i, carried):
        kind, s = i // 2, lax.rem(i, 2)
        for h in range(2):
            arrive(4 * kind + 2 * s + h)
        wait_carry(kind, s)
        for t in range(ext // TILE):
            span = slice(TILE * t, TILE * t + TILE)
            where = slice(PAD + TILE * t, PAD + TILE * t + TILE)
            for c in range(2):
                u2[c, where] = carry[kind, s, c, span]
                u2[2 + c, where] = unfold(carry_side[kind, s, 0, c], carry_side[kind, s, 1, c], t)

        def plane(j, inner):
            z = jnp.where(kind == 0, j, 2 * planes - 1 - j)
            h, p = z // planes, lax.rem(z, planes)
            g = 4 * kind + 2 * s + h
            for t in range(ext // TILE):
                span = slice(TILE * t, TILE * t + TILE)
                where = slice(PAD + TILE * t, PAD + TILE * t + TILE)
                for c in range(2):
                    held[c, span] = data[g, 2 * p + c, span] + 2.5 * u2[c, where]
                    held[2 + c, span] = side_of(g, p, c, t) + 2.5 * u2[2 + c, where]
            relax(kind, s, z)
            return inner

        lax.fori_loop(0, 2 * planes, plane, 0)
        hand_on(kind, s)

        @pl.when(kind == 0)
        def _():
            ref = observed.at[s, 1 - half]
            remote(ref, ref, obs_send.at[s], obs_recv.at[s], anyone).wait_recv()
            for h in (1, 0):
                g = residual_group(s, h)
                for p in range(planes):
                    for c in range(2):
                        data[g, 2 * p + c, halo : halo + rows] = (
                            result[0, s, planes * h + p, c] - observed[s, h, 2 * p + c]
                        )
                exchange(g)
            field_out(s, True).start()
            pltpu.make_async_copy(
                result.at[0, s, pl.ds(planes * half, planes)], fout.at[:, :, mine + s], load.at[s]
            ).start()

        @pl.when(kind == 1)
        def _():
            for z in range(2 * planes):
                value = total[z]
                for c in range(2):
                    value = value + result[0, s, z, c] * result[1, s, z, c]
                total[z] = value

        return carried

    lax.fori_loop(0, 4, step, 0)
    remote(
        total.at[pl.ds(planes * (1 - half), planes)], other, grad_send.at[0], grad_recv.at[0], partner
    ).start()

    def finish(g, carried):
        remote(edges(g), edges(g), row_send.at[g], row_recv.at[g], anyone).wait_send()
        remote(sides.at[g], sides.at[g], side_send.at[g], side_recv.at[g], anyone).wait_send()
        return carried

    lax.fori_loop(0, 10, finish, 0)
    whole = data.at[0, :, block]
    for k in range(3):
        remote(whole, whole, in_send.at[k], in_recv.at[k], anyone).wait_send()
    for s in range(2):
        ref = observed.at[s, 0]
        remote(ref, ref, obs_send.at[s], obs_recv.at[s], anyone).wait_send()
        ref = result.at[0, s, pl.ds(planes * (1 - half), planes)]
        remote(ref, ref, out_send.at[s], out_recv.at[s], anyone).wait_send()
        remote(ref, ref, out_send.at[s], out_recv.at[s], anyone).wait_recv()
        pltpu.make_async_copy(
            result.at[0, s, pl.ds(planes * half, planes)], fout.at[:, :, mine + s], load.at[s]
        ).wait()
        for kind in range(2):

            @pl.when(kind == lower)
            def _():
                side, main = leave_side.at[kind, s], leave.at[kind, s, :, most]
                remote(side, side, cside_send.at[kind, s], cside_recv.at[kind, s], anyone).wait_send()
                remote(main, main, carry_send.at[kind, s], carry_recv.at[kind, s], anyone).wait_send()

    sent = remote(other, other, grad_send.at[0], grad_recv.at[0], anyone)
    sent.wait_recv()
    held[0:planes, 0:rows] = (total[pl.ds(planes * half, planes)] + other[...]) * (1.0 / shots)
    pltpu.sync_copy(held.at[0:planes, 0:rows], gout)
    sent.wait_send()


def body(sizes, source, observed, wavenumber, damping):
    planes, comps, shots, rows, lanes = source.shape
    ndepth = sizes[0]
    edge = 4 * planes
    halo = 2 * edge
    ext = rows + 2 * halo
    assert comps == 2 and planes == 2 and shots == 4 and ndepth == 4
    assert lanes == LANES and edge * 2 * rows == TILE * LANES
    vmem = lambda *shape: pltpu.VMEM(shape, jnp.float32)
    dma = lambda *shape: pltpu.SemaphoreType.DMA(shape)
    anywhere = pl.BlockSpec(memory_space=pl.ANY)
    return pl.pallas_call(
        functools.partial(kernel, sizes, halo, edge),
        name="sweeps",
        out_shape=(
            jax.ShapeDtypeStruct(source.shape, jnp.float32),
            jax.ShapeDtypeStruct(wavenumber.shape, jnp.float32),
        ),
        in_specs=[anywhere] * 4,
        out_specs=(anywhere, anywhere),
        scratch_shapes=[
            vmem(10, 4, ext, lanes),
            vmem(10, 2, 3, 2, TILE, lanes),
            vmem(10, 2, 2, TILE, lanes),
            vmem(2, 2, 4, rows, lanes),
            vmem(2, 4, 4, ext, lanes),
            vmem(2, 2, 2, ext, lanes),
            vmem(2, 2, 2, 2, TILE, lanes),
            vmem(2, 2, 2, ext, lanes),
            vmem(2, 2, 2, 2, TILE, lanes),
            vmem(2, 2, 4, 2, rows, lanes),
            vmem(4, ext + 2 * PAD, lanes),
            vmem(4, ext + 2 * PAD, lanes),
            vmem(4, ext + 2 * PAD, lanes),
            vmem(4, ext, lanes),
            vmem(4, rows, lanes),
            vmem(2, rows, lanes),
            dma(10),
            dma(10),
            dma(10),
            dma(10),
            dma(10),
            dma(2, 2),
            dma(2, 2),
            dma(2, 2),
            dma(2, 2),
            dma(3),
            dma(3),
            dma(2),
            dma(2),
            dma(2),
            dma(2),
            dma(1),
            dma(1),
        ],
        compiler_params=pltpu.CompilerParams(
            collective_id=0, has_side_effects=True, vmem_limit_bytes=60 << 20
        ),
    )(source, observed, wavenumber, damping)


def solution(mesh):
    sizes = tuple(mesh.shape[axis] for axis in ("depth", "gx", "gy"))
    return jax.shard_map(
        functools.partial(body, sizes),
        mesh=mesh,
        in_specs=(
            P("depth", None, None, "gx", "gy"),
            P("depth", None, None, "gx", "gy"),
            P("depth", "gx", "gy"),
            P("depth", "gx", "gy"),
        ),
        out_specs=(P("depth", None, None, "gx", "gy"), P("depth", "gx", "gy")),
        check_vma=False,
    )
```

time: 737 us -> 70.2 us (0.10); the launches traced: 723 us -> 70 us
  starting transfers between devices: 409 us -> 0 us
  waiting for transfers between devices: 287 us -> 0 us
  Pallas kernels: 0 us -> 66.8 us
  other arithmetic: 16.4 us -> 0 us
    ppermute x134 -> x0, starting transfers between devices: 409 us -> none  [the longest x64 279 us: with_halo(): lax.ppermute(tail, axis, [(i, (i + 1) % count) for i in range(ends)])]
    ppermute x134 -> x0, waiting for transfers between devices: 287 us -> none  [the longest x64 126 us: with_halo(): lax.ppermute(head, axis, [((i + 1) % count, i) for i in range(ends)])]
    pallas_call x0 -> x1, Pallas kernels: none -> 66.8 us  [body(): pl.pallas_call(functools.partial(kernel, sizes, halo, edge), name='sweeps...]
    add x48 -> x0, other arithmetic: 9.86 us -> none  [the longest x32 9.26 us: relax(): field = complex_scale(drive + beside, inverse)]
  transfers between devices with their start and end apart: 134 -> 0, of which waited for: 102 -> 0; matrix products, arithmetic and copies ran while one was open for 0% -> 0% of each run, Pallas kernels for 0% -> 0%
where the time goes in v2:
time: 70.2 us; the launch traced here: 70 us
  Pallas kernels  66.8 us (95%)
  local copies, waits for them, and re-layouts  2.55 us (4%)
    pallas_call x1, Pallas kernels, body(): pl.pallas_call(functools.partial(kernel, sizes, halo, edge), name='sweeps...  66.8 us
    unnamed x4, local copies, waits for them, and re-layouts  2.55 us

profile of v2, /device:TPU:1, one launch (start us, length us, event | category | flops | bytes accessed | tf_op | source)
XLA Modules:
  0.0 70.0 jit_solution(873335066916725352)
XLA Ops:
  0.6 66.8 %sweeps.1 = (f32[2,2,4,64,128]{4,3,2,1,0:T(8,128)}, f32[2,64,128]{2,1,0:T(8,128)}) custom-call(f32[2,2,4,64,128]{4,3,2,1,0:T(8,128)} %src.1, f32[2,2,4,64,128]{4,3,2,1,0:T(8,128)} %obs.1, f32[2,64,128]{2,1,0:T(8,128)} %wavenumber.1, f32[2,64,128]{2,1,0:T(8,128)} %damping.1), custom_call_target="tpu_custom_call" | custom-call | tf_op jit(solution)/shard_map/sweeps/pallas_call | solution.py:495
  67.5 0.0 copy-start
  67.5 1.9 %copy.8 = f32[2,2,4,64,128]{4,3,2,1,0:T(8,128)} copy(f32[2,2,4,64,128]{4,3,2,1,0:T(8,128)} %get-tuple-element.4) | data formatting | bytes 1048576
  69.4 0.0 copy-done
  69.4 0.6 copy.9
Async XLA Ops:
  67.5 1.9 %copy-start = (f32[2,64,128]{2,1,0:T(8,128)S(1)}, f32[2,64,128]{2,1,0:T(8,128)}, u32[]{:S(2)}) copy-start(f32[2,64,128]{2,1,0:T(8,128)} %get-tuple-element.5) | copy-start | bytes 196612

commit v3 on v2

--- a/solution.py
+++ b/solution.py
@@ -98,6 +98,11 @@
     through = [{"depth": ndepth - 1 - d, "gy": y} for y in (b, left, right)]
     anyone = beside[0]
 
+    barrier = pltpu.get_barrier_semaphore()
+    partners = beside + [partner] + through
+    for device in partners:
+        pl.semaphore_signal(barrier, inc=1, device_id=device, device_id_type=MESH)
+
     def remote(source, target, send, recv, device):
         return pltpu.make_async_remote_copy(
             src_ref=source,
@@ -130,14 +135,6 @@
     for copy in inverse_loads + source_loads + observed_loads:
         copy.start()
 
-    carry[...] = jnp.zeros_like(carry)
-    carry_side[...] = jnp.zeros_like(carry_side)
-
-    barrier = pltpu.get_barrier_semaphore()
-    partners = beside + [partner] + through
-    for device in partners:
-        pl.semaphore_signal(barrier, inc=1, device_id=device, device_id_type=MESH)
-
     for copy in inverse_loads:
         copy.wait()
     for p in range(planes):
@@ -167,6 +164,15 @@
         u2[k, 0:PAD] = jnp.zeros_like(u2[k, 0:PAD])
         u2[k, PAD + ext : 2 * PAD + ext] = jnp.zeros_like(u2[k, 0:PAD])
     total[...] = jnp.zeros_like(total)
+    none = jnp.zeros((TILE, LANES), jnp.float32)
+    for s in range(2):
+        for c in range(2):
+            for t in range(ext // TILE):
+                carry[lower, s, c, TILE * t : TILE * t + TILE] = none
+            carry[1 - lower, s, c, 0:TILE] = none
+            carry[1 - lower, s, c, ext - TILE : ext] = none
+            for side in range(2):
+                carry_side[lower, s, side, c] = none
 
     lane = lax.broadcasted_iota(jnp.int32, (TILE, LANES), 1)
     lane_group = lane // edge
@@ -246,6 +252,17 @@
         remote(whole, whole, in_send.at[k], in_recv.at[k], anyone).wait_recv()
         exchange(g)
 
+    def send_observed():
+        for s in range(2):
+            for p in range(planes):
+                remote(
+                    obs.at[p, :, theirs + s],
+                    observed.at[s, half, pl.ds(2 * p, 2)],
+                    obs_send.at[s],
+                    obs_recv.at[s],
+                    partner,
+                ).start()
+
     def spread(i, c):
         @pl.when(i < 2)
         def _():
@@ -255,19 +272,13 @@
         def _():
             landed(i - 2, jnp.where(i == 2, inverse_group(1 - half), source_group(i - 3, 1 - half)))
 
+        @pl.when(i == 4)
+        def _():
+            send_observed()
+
         return c
 
     lax.fori_loop(0, 5, spread, 0)
-    for s in range(2):
-        for p in range(planes):
-            remote(
-                obs.at[p, :, theirs + s],
-                observed.at[s, half, pl.ds(2 * p, 2)],
-                obs_send.at[s],
-                obs_recv.at[s],
-                partner,
-            ).start()
-
     not_top = (a > 0).astype(jnp.float32)
     not_bottom = (a < ngx - 1).astype(jnp.float32)
     not_left = (b > 0).astype(jnp.float32)
@@ -384,14 +395,21 @@
                 through[0],
             ).start()
 
-    def field_out(s, send):
-        mine_now = result.at[0, s, pl.ds(planes * (1 - half), planes)]
-        return remote(mine_now, fout.at[:, :, mine + s], out_send.at[s], out_recv.at[s], partner)
+    def field_out(s):
+        away = result.at[0, s, pl.ds(planes * (1 - half), planes)]
+        remote(away, fout.at[:, :, mine + s], out_send.at[s], out_recv.at[s], partner).start()
+        here = result.at[0, s, pl.ds(planes * half, planes)]
+        pltpu.make_async_copy(here, fout.at[:, :, mine + s], load.at[s]).start()
 
     def step(i, carried):
         kind, s = i // 2, lax.rem(i, 2)
         for h in range(2):
             arrive(4 * kind + 2 * s + h)
+
+        @pl.when(kind == 1)
+        def _():
+            field_out(s)
+
         wait_carry(kind, s)
         for t in range(ext // TILE):
             span = slice(TILE * t, TILE * t + TILE)
@@ -411,6 +429,18 @@
                     held[c, span] = data[g, 2 * p + c, span] + 2.5 * u2[c, where]
                     held[2 + c, span] = side_of(g, p, c, t) + 2.5 * u2[2 + c, where]
             relax(kind, s, z)
+
+            @pl.when(kind == 1)
+            def _():
+                value = total[z]
+                for c in range(2):
+                    value = value + result[0, s, z, c] * result[1, s, z, c]
+                total[z] = value
+
+            @pl.when((i == 3) & (h != half))
+            def _():
+                remote(total.at[z], other.at[p], grad_send.at[p], grad_recv.at[p], partner).start()
+
             return inner
 
         lax.fori_loop(0, 2 * planes, plane, 0)
@@ -428,25 +458,10 @@
                             result[0, s, planes * h + p, c] - observed[s, h, 2 * p + c]
                         )
                 exchange(g)
-            field_out(s, True).start()
-            pltpu.make_async_copy(
-                result.at[0, s, pl.ds(planes * half, planes)], fout.at[:, :, mine + s], load.at[s]
-            ).start()
-
-        @pl.when(kind == 1)
-        def _():
-            for z in range(2 * planes):
-                value = total[z]
-                for c in range(2):
-                    value = value + result[0, s, z, c] * result[1, s, z, c]
-                total[z] = value
 
         return carried
 
     lax.fori_loop(0, 4, step, 0)
-    remote(
-        total.at[pl.ds(planes * (1 - half), planes)], other, grad_send.at[0], grad_recv.at[0], partner
-    ).start()
 
     def finish(g, carried):
         remote(edges(g), edges(g), row_send.at[g], row_recv.at[g], anyone).wait_send()
@@ -474,11 +489,13 @@
                 remote(side, side, cside_send.at[kind, s], cside_recv.at[kind, s], anyone).wait_send()
                 remote(main, main, carry_send.at[kind, s], carry_recv.at[kind, s], anyone).wait_send()
 
-    sent = remote(other, other, grad_send.at[0], grad_recv.at[0], anyone)
-    sent.wait_recv()
+    sent = [remote(other.at[p], other.at[p], grad_send.at[p], grad_recv.at[p], anyone) for p in range(planes)]
+    for copy in sent:
+        copy.wait_recv()
     held[0:planes, 0:rows] = (total[pl.ds(planes * half, planes)] + other[...]) * (1.0 / shots)
     pltpu.sync_copy(held.at[0:planes, 0:rows], gout)
-    sent.wait_send()
+    for copy in sent:
+        copy.wait_send()
 
 
 def body(sizes, source, observed, wavenumber, damping):
@@ -533,13 +550,13 @@
             dma(2),
             dma(2),
             dma(2),
-            dma(1),
-            dma(1),
+            dma(2),
+            dma(2),
         ],
         compiler_params=pltpu.CompilerParams(
-            collective_id=0, has_side_effects=True, vmem_limit_bytes=60 << 20
+            collective_id=0, has_side_effects=True, vmem_limit_bytes=24 << 20
         ),
-    )(source, observed, wavenumber, damping)
+    )(*(pltpu.with_memory_space_constraint(x, pltpu.HBM) for x in (source, observed, wavenumber, damping)))
 
 
 def solution(mesh):

time: 70.2 us -> 67.6 us (0.963)
  Pallas kernels: 66.8 us -> 65.5 us
  local copies, waits for them, and re-layouts: 2.55 us -> 1.42 us
    pallas_call x1, Pallas kernels: 66.8 us -> 65.5 us  [body(): pl.pallas_call(functools.partial(kernel, sizes, halo, edge), name='sweeps...]
    unnamed x4 -> x2, local copies, waits for them, and re-layouts: 2.55 us -> 1.42 us
where the time goes in v3:
time: 67.6 us; the launch traced here: 67.5 us
  Pallas kernels  65.5 us (97%)
  local copies, waits for them, and re-layouts  1.42 us (2%)
    pallas_call x1, Pallas kernels, body(): pl.pallas_call(functools.partial(kernel, sizes, halo, edge), name='sweeps...  65.5 us
    unnamed x2, local copies, waits for them, and re-layouts  1.42 us

profile of v3, /device:TPU:1, one launch (start us, length us, event | category | flops | bytes accessed | tf_op | source)
XLA Modules:
  0.0 67.5 jit_solution(2616663780025720274)
XLA Ops:
  0.6 65.5 %sweeps.1 = (f32[2,2,4,64,128]{4,3,2,1,0:T(8,128)S(1)}, f32[2,64,128]{2,1,0:T(8,128)S(1)}) custom-call(f32[2,2,4,64,128]{4,3,2,1,0:T(8,128)} %src.1, f32[2,2,4,64,128]{4,3,2,1,0:T(8,128)} %obs.1, f32[2,64,128]{2,1,0:T(8,128)} %wavenumber.1, f32[2,64,128]{2,1,0:T(8,128)} %damping.1), custom_call_target="tpu_custom_call" | custom-call | tf_op jit(solution)/shard_map/sweeps/pallas_call | solution.py:512
  66.1 0.8 %copy.8 = f32[2,2,4,64,128]{4,3,2,1,0:T(8,128)} copy(f32[2,2,4,64,128]{4,3,2,1,0:T(8,128)S(1)} %get-tuple-element.4) | data formatting | bytes 1048576
  66.9 0.6 copy.9

commit v4 on v3

--- a/solution.py
+++ b/solution.py
@@ -401,12 +401,25 @@
         here = result.at[0, s, pl.ds(planes * half, planes)]
         pltpu.make_async_copy(here, fout.at[:, :, mine + s], load.at[s]).start()
 
+    def remain(s, carried):
+        ref = observed.at[s, 1 - half]
+        remote(ref, ref, obs_send.at[s], obs_recv.at[s], anyone).wait_recv()
+        for h in (1, 0):
+            g = residual_group(s, h)
+            for p in range(planes):
+                for c in range(2):
+                    data[g, 2 * p + c, halo : halo + rows] = (
+                        result[0, s, planes * h + p, c] - observed[s, h, 2 * p + c]
+                    )
+            exchange(g)
+        return carried
+
     def step(i, carried):
         kind, s = i // 2, lax.rem(i, 2)
         for h in range(2):
             arrive(4 * kind + 2 * s + h)
 
-        @pl.when(kind == 1)
+        @pl.when((kind == 1) & (lower == 0))
         def _():
             field_out(s)
 
@@ -446,18 +459,15 @@
         lax.fori_loop(0, 2 * planes, plane, 0)
         hand_on(kind, s)
 
+        @pl.when((kind == 1) & (lower == 1))
+        def _():
+            field_out(s)
+
         @pl.when(kind == 0)
         def _():
-            ref = observed.at[s, 1 - half]
-            remote(ref, ref, obs_send.at[s], obs_recv.at[s], anyone).wait_recv()
-            for h in (1, 0):
-                g = residual_group(s, h)
-                for p in range(planes):
-                    for c in range(2):
-                        data[g, 2 * p + c, halo : halo + rows] = (
-                            result[0, s, planes * h + p, c] - observed[s, h, 2 * p + c]
-                        )
-                exchange(g)
+            start = jnp.where(lower == 1, s, 0)
+            end = jnp.where(lower == 1, s + 1, 2 * s)
+            lax.fori_loop(start, end, remain, 0)
 
         return carried
 

time: 67.6 us -> 67 us (level)
  the two profiles are of different devices: /device:TPU:1 before, /device:TPU:6 now
where the time goes in v4:
time: 67 us; the launch traced here: 66.9 us
  Pallas kernels  64.8 us (97%)
  local copies, waits for them, and re-layouts  1.42 us (2%)
    pallas_call x1, Pallas kernels, body(): pl.pallas_call(functools.partial(kernel, sizes, halo, edge), name='sweeps...  64.8 us
    unnamed x2, local copies, waits for them, and re-layouts  1.42 us

profile of v4, /device:TPU:6, one launch (start us, length us, event | category | flops | bytes accessed | tf_op | source)
XLA Modules:
  0.0 66.9 jit_solution(3262635275399910356)
XLA Ops:
  0.6 64.8 %sweeps.1 = (f32[2,2,4,64,128]{4,3,2,1,0:T(8,128)S(1)}, f32[2,64,128]{2,1,0:T(8,128)S(1)}) custom-call(f32[2,2,4,64,128]{4,3,2,1,0:T(8,128)} %src.1, f32[2,2,4,64,128]{4,3,2,1,0:T(8,128)} %obs.1, f32[2,64,128]{2,1,0:T(8,128)} %wavenumber.1, f32[2,64,128]{2,1,0:T(8,128)} %damping.1), custom_call_target="tpu_custom_call" | custom-call | tf_op jit(solution)/shard_map/sweeps/pallas_call | solution.py:522
  65.4 0.8 %copy.8 = f32[2,2,4,64,128]{4,3,2,1,0:T(8,128)} copy(f32[2,2,4,64,128]{4,3,2,1,0:T(8,128)S(1)} %get-tuple-element.4) | data formatting | bytes 1048576
  66.2 0.6 copy.9

commit v5 on v4

--- a/solution.py
+++ b/solution.py
@@ -272,7 +272,7 @@
         def _():
             landed(i - 2, jnp.where(i == 2, inverse_group(1 - half), source_group(i - 3, 1 - half)))
 
-        @pl.when(i == 4)
+        @pl.when((i == 4) & (lower == 1))
         def _():
             send_observed()
 
@@ -419,10 +419,6 @@
         for h in range(2):
             arrive(4 * kind + 2 * s + h)
 
-        @pl.when((kind == 1) & (lower == 0))
-        def _():
-            field_out(s)
-
         wait_carry(kind, s)
         for t in range(ext // TILE):
             span = slice(TILE * t, TILE * t + TILE)
@@ -465,6 +461,12 @@
 
         @pl.when(kind == 0)
         def _():
+            @pl.when((lower == 0) & (s == 1))
+            def _():
+                send_observed()
+                for q in range(2):
+                    field_out(q)
+
             start = jnp.where(lower == 1, s, 0)
             end = jnp.where(lower == 1, s + 1, 2 * s)
             lax.fori_loop(start, end, remain, 0)

time: 67 us -> 66.2 us (0.988)
  the two profiles are of different devices: /device:TPU:6 before, /device:TPU:1 now
where the time goes in v5:
time: 66.2 us; the launch traced here: 65.3 us
  Pallas kernels  63.3 us (96%)
  local copies, waits for them, and re-layouts  1.42 us (2%)
    pallas_call x1, Pallas kernels, body(): pl.pallas_call(functools.partial(kernel, sizes, halo, edge), name='sweeps...  63.3 us
    unnamed x2, local copies, waits for them, and re-layouts  1.42 us

profile of v5, /device:TPU:1, one launch (start us, length us, event | category | flops | bytes accessed | tf_op | source)
XLA Modules:
  0.0 65.3 jit_solution(18028871982935552268)
XLA Ops:
  0.6 63.3 %sweeps.1 = (f32[2,2,4,64,128]{4,3,2,1,0:T(8,128)S(1)}, f32[2,64,128]{2,1,0:T(8,128)S(1)}) custom-call(f32[2,2,4,64,128]{4,3,2,1,0:T(8,128)} %src.1, f32[2,2,4,64,128]{4,3,2,1,0:T(8,128)} %obs.1, f32[2,64,128]{2,1,0:T(8,128)} %wavenumber.1, f32[2,64,128]{2,1,0:T(8,128)} %damping.1), custom_call_target="tpu_custom_call" | custom-call | tf_op jit(solution)/shard_map/sweeps/pallas_call | solution.py:524
  63.9 0.8 %copy.8 = f32[2,2,4,64,128]{4,3,2,1,0:T(8,128)} copy(f32[2,2,4,64,128]{4,3,2,1,0:T(8,128)S(1)} %get-tuple-element.4) | data formatting | bytes 1048576
  64.7 0.6 copy.9

commit v6 on v5

--- a/solution.py
+++ b/solution.py
@@ -146,6 +146,17 @@
 
     pl.semaphore_wait(barrier, len(partners))
 
+    def send_observed():
+        for s in range(2):
+            for p in range(planes):
+                remote(
+                    obs.at[p, :, theirs + s],
+                    observed.at[s, half, pl.ds(2 * p, 2)],
+                    obs_send.at[s],
+                    obs_recv.at[s],
+                    partner,
+                ).start()
+
     own_inverse = data.at[inverse_group(half), :, block]
     remote(own_inverse, own_inverse, in_send.at[0], in_recv.at[0], partner).start()
     for s in range(2):
@@ -157,6 +168,10 @@
                 in_recv.at[1 + s],
                 partner,
             ).start()
+
+    @pl.when(lower == 1)
+    def _():
+        send_observed()
 
     for u in (u0, u1):
         u[...] = jnp.zeros_like(u)
@@ -252,17 +267,6 @@
         remote(whole, whole, in_send.at[k], in_recv.at[k], anyone).wait_recv()
         exchange(g)
 
-    def send_observed():
-        for s in range(2):
-            for p in range(planes):
-                remote(
-                    obs.at[p, :, theirs + s],
-                    observed.at[s, half, pl.ds(2 * p, 2)],
-                    obs_send.at[s],
-                    obs_recv.at[s],
-                    partner,
-                ).start()
-
     def spread(i, c):
         @pl.when(i < 2)
         def _():
@@ -271,10 +275,6 @@
         @pl.when(i >= 2)
         def _():
             landed(i - 2, jnp.where(i == 2, inverse_group(1 - half), source_group(i - 3, 1 - half)))
-
-        @pl.when((i == 4) & (lower == 1))
-        def _():
-            send_observed()
 
         return c
 

time: 66.2 us -> 66.2 us (level)
  no operation moved by 1% of the time
where the time goes in v6:
time: 66.2 us; the launch traced here: 65.3 us
  Pallas kernels  63.3 us (96%)
  local copies, waits for them, and re-layouts  1.42 us (2%)
    pallas_call x1, Pallas kernels, body(): pl.pallas_call(functools.partial(kernel, sizes, halo, edge), name='sweeps...  63.3 us
    unnamed x2, local copies, waits for them, and re-layouts  1.42 us

profile of v6, /device:TPU:1, one launch (start us, length us, event | category | flops | bytes accessed | tf_op | source)
XLA Modules:
  0.0 65.3 jit_solution(10600684018150822930)
XLA Ops:
  0.6 63.3 %sweeps.1 = (f32[2,2,4,64,128]{4,3,2,1,0:T(8,128)S(1)}, f32[2,64,128]{2,1,0:T(8,128)S(1)}) custom-call(f32[2,2,4,64,128]{4,3,2,1,0:T(8,128)} %src.1, f32[2,2,4,64,128]{4,3,2,1,0:T(8,128)} %obs.1, f32[2,64,128]{2,1,0:T(8,128)} %wavenumber.1, f32[2,64,128]{2,1,0:T(8,128)} %damping.1), custom_call_target="tpu_custom_call" | custom-call | tf_op jit(solution)/shard_map/sweeps/pallas_call | solution.py:524
  63.9 0.8 %copy.8 = f32[2,2,4,64,128]{4,3,2,1,0:T(8,128)} copy(f32[2,2,4,64,128]{4,3,2,1,0:T(8,128)S(1)} %get-tuple-element.4) | data formatting | bytes 1048576
  64.7 0.6 copy.9

commit v7 on v6

--- a/solution.py
+++ b/solution.py
@@ -387,13 +387,14 @@
                     cside_recv.at[kind, s],
                     device,
                 ).start()
-            remote(
-                leave.at[kind, s, :, most],
-                carry.at[kind, s, :, most],
-                carry_send.at[kind, s],
-                carry_recv.at[kind, s],
-                through[0],
-            ).start()
+            for c in range(2):
+                remote(
+                    leave.at[kind, s, c, most],
+                    carry.at[kind, s, c, most],
+                    carry_send.at[kind, s],
+                    carry_recv.at[kind, s],
+                    through[0],
+                ).start()
 
     def field_out(s):
         away = result.at[0, s, pl.ds(planes * (1 - half), planes)]

time: 66.2 us -> 66.1 us (level)
  no operation moved by 1% of the time
where the time goes in v7:
time: 66.1 us; the launch traced here: 65.4 us
  Pallas kernels  63.3 us (96%)
  local copies, waits for them, and re-layouts  1.42 us (2%)
    pallas_call x1, Pallas kernels, body(): pl.pallas_call(functools.partial(kernel, sizes, halo, edge), name='sweeps...  63.3 us
    unnamed x2, local copies, waits for them, and re-layouts  1.42 us

profile of v7, /device:TPU:1, one launch (start us, length us, event | category | flops | bytes accessed | tf_op | source)
XLA Modules:
  0.0 65.4 jit_solution(2770607353661913426)
XLA Ops:
  0.6 63.3 %sweeps.1 = (f32[2,2,4,64,128]{4,3,2,1,0:T(8,128)S(1)}, f32[2,64,128]{2,1,0:T(8,128)S(1)}) custom-call(f32[2,2,4,64,128]{4,3,2,1,0:T(8,128)} %src.1, f32[2,2,4,64,128]{4,3,2,1,0:T(8,128)} %obs.1, f32[2,64,128]{2,1,0:T(8,128)} %wavenumber.1, f32[2,64,128]{2,1,0:T(8,128)} %damping.1), custom_call_target="tpu_custom_call" | custom-call | tf_op jit(solution)/shard_map/sweeps/pallas_call | solution.py:525
  64.0 0.8 %copy.8 = f32[2,2,4,64,128]{4,3,2,1,0:T(8,128)} copy(f32[2,2,4,64,128]{4,3,2,1,0:T(8,128)S(1)} %get-tuple-element.4) | data formatting | bytes 1048576
  64.8 0.6 copy.9
